TPU v7x, 32 devices: a whole 2x2x4 slice. The times are simulated.
32 devices in a mesh: lat: 4 (over z), lon: 8 (over y, x, core).
Axes of the slice: x: 2, y: 2, z: 4, core: 2. Of those that a mesh axis runs over, the one named last changes fastest.
Arguments:
- mesh_latent: bfloat16 [32, 64, 512], P('lat', 'lon'), may hold values from -6 to 6
- grid_cotangent: bfloat16 [32768, 512], P(('lat', 'lon')), may hold values from -6 to 6
- w_source: bfloat16 [512, 512], replicated, may hold values from -0.25 to 0.25
- w_target: bfloat16 [512, 512], replicated, may hold values from -0.25 to 0.25
- w_node: bfloat16 [512, 512], replicated, may hold values from -0.25 to 0.25
- w_coarse: bfloat16 [512, 512], replicated, may hold values from -0.25 to 0.25
- w_decode: bfloat16 [512, 512], replicated, may hold values from -0.25 to 0.25
- neighbour_codes: int32 [6, 32, 64], P(None, 'lat', 'lon'), may hold values from 0 to 8, as said below
- coarse_ids: int32 [32, 64, 1], P('lat', 'lon'), may hold values from 0 to 641
- edge_source: int32 [98304], P(('lat', 'lon')), may hold values from 0 to 63
- edge_target: int32 [98304], P(('lat', 'lon')), may hold values from 0 to 1023
- edge_owner: int32 [768, 1], P(('lat', 'lon')), may hold values from 0 to 7, as said below
Outputs:
- mesh_out: bfloat16 [32, 64, 512], P('lat', 'lon')
- grid_out: bfloat16 [32768, 512], P(('lat', 'lon'))
- clipped: float32 [5, 262144], P(None, ('lat', 'lon'))
Inputs may be any that keep to these rules, and one draw needn't show every extreme that they name: `neighbour_codes`: code c names the row offset c // 3 - 1 and the column offset c % 3 - 1 and is never 4; the six codes of one node differ. `coarse_ids`: every coarse node has at least one mesh node. `edge_owner`: the owner of a block held by the device at longitude index b is b, or b - 1 or b + 1 on the periodic cycle of longitude indices. Among the 24 blocks of one device at most 3 name b - 1 and at most 3 name b + 1; in every draw some device receives 3 blocks from each of its two neighbours.
All inputs are finite; a program needn't handle non-finite values.
Results may differ from a plain program's by a relative error of at most 0.008.
Values may be sent and summed in bfloat16 or wider, within the bound.
A program may use at most 64 MiB of HBM per device.

v0:
```python
import jax
import jax.numpy as jnp
from jax import lax
from jax.sharding import PartitionSpec as P

COARSE = 642
CAP = 3


def padded_2(cells, sides, width):
    for axis, dim in sides:
        count = lax.axis_size(axis)
        head = lax.slice_in_dim(cells, 0, width, axis=dim)
        tail = lax.slice_in_dim(cells, cells.shape[dim] - width, cells.shape[dim], axis=dim)
        cells = jnp.concatenate(
            [
                lax.ppermute(tail, axis, [(i, (i + 1) % count) for i in range(count)]),
                cells,
                lax.ppermute(head, axis, [((i + 1) % count, i) for i in range(count)]),
            ],
            axis=dim,
        )
    return cells


def silu_slope(value):
    sig = jax.nn.sigmoid(value)
    return sig * (1.0 + value * (1.0 - sig))


def hot_table(indices, length):
    return (indices[:, None] == jnp.arange(length, dtype=jnp.int32)[None, :]).astype(jnp.bfloat16)


def contract_first(left, right):
    return lax.dot_general(
        left, right, (((0,), (0,)), ((), ())), preferred_element_type=jnp.float32
    )


def local(
    mesh_latent,
    grid_cotangent,
    w_source,
    w_target,
    w_node,
    w_coarse,
    w_decode,
    neighbour_codes,
    coarse_ids,
    edge_source,
    edge_target,
    edge_owner,
):
    height, breadth, width = mesh_latent.shape
    nodes = height * breadth
    padded = padded_2(mesh_latent, (("lat", 0), ("lon", 1)), 1)
    lat_pos = lax.axis_index("lat")
    lat_count = lax.axis_size("lat")
    row_ids = jnp.arange(height + 2, dtype=jnp.int32)
    outside = (row_ids == 0) & (lat_pos == 0) | (row_ids == height + 1) & (lat_pos == lat_count - 1)
    padded = jnp.where(outside[:, None, None], jnp.zeros_like(padded), padded)
    flat_pad = padded.reshape(-1, width)
    row_at = jnp.arange(height, dtype=jnp.int32)[None, :, None] + neighbour_codes // 3
    col_at = jnp.arange(breadth, dtype=jnp.int32)[None, None, :] + neighbour_codes % 3
    where_idx = (row_at * (breadth + 2) + col_at).reshape(-1)
    beside = jnp.dot(
        hot_table(where_idx, flat_pad.shape[0]), flat_pad, preferred_element_type=jnp.float32
    ).astype(jnp.bfloat16)
    latent = mesh_latent.reshape(nodes, width)
    toward = jnp.dot(latent, w_target, preferred_element_type=jnp.float32)
    edges_pre = (
        jnp.dot(beside, w_source, preferred_element_type=jnp.float32).reshape(6, nodes, width)
        + toward[None]
    )
    agg = jnp.sum(jax.nn.silu(edges_pre), 0).astype(jnp.bfloat16)
    onehot = (coarse_ids.reshape(nodes, 1) == jnp.arange(COARSE, dtype=jnp.int32)[None]).astype(
        jnp.bfloat16
    )
    pooled_part = jnp.dot(onehot.T, latent, preferred_element_type=jnp.float32)
    count_part = jnp.sum(onehot.astype(jnp.float32), 0)
    pooled, count = lax.psum((pooled_part, count_part), ("lat", "lon"))
    coarse_in = (pooled * lax.rsqrt(count)[:, None]).astype(jnp.bfloat16)
    cpre = jnp.dot(coarse_in, w_coarse, preferred_element_type=jnp.float32)
    coarse_out = jax.nn.silu(cpre).astype(jnp.bfloat16)
    child = jnp.dot(onehot, coarse_out, preferred_element_type=jnp.float32)
    npre = jnp.dot(agg, w_node, preferred_element_type=jnp.float32) + child
    mesh_out = (latent.astype(jnp.float32) + jax.nn.silu(npre)).astype(jnp.bfloat16)
    lon_pos = lax.axis_index("lon")
    lon_count = lax.axis_size("lon")
    blocks = edge_owner.shape[0]
    block_len = edge_source.shape[0] // blocks
    grid_rows = grid_cotangent.shape[0]
    owner_vec = edge_owner[:, 0]
    side = (owner_vec - lon_pos + lon_count) % lon_count
    to_left = (side == lon_count - 1).astype(jnp.int32)
    to_right = (side == 1).astype(jnp.int32)
    stays = side == 0
    left_rank = jnp.cumsum(to_left) - to_left
    right_rank = jnp.cumsum(to_right) - to_right
    place = jnp.where(to_left == 1, left_rank, jnp.where(to_right == 1, CAP + right_rank, -1))
    placing = jnp.arange(2 * CAP, dtype=jnp.int32)[:, None] == place[None, :]
    placing_int = placing.astype(jnp.int32)
    placing_bf = placing.astype(jnp.bfloat16)
    target_grid = edge_target.reshape(blocks, block_len)
    own_target = jnp.where(stays[:, None], target_grid, grid_rows).reshape(-1)
    own_edges = blocks * block_len
    source_hot = hot_table(edge_source, nodes)
    gathered = jnp.dot(source_hot, mesh_out, preferred_element_type=jnp.float32).astype(
        jnp.bfloat16
    )
    pre = jnp.dot(gathered, w_decode, preferred_element_type=jnp.float32)
    message = jax.nn.silu(pre).astype(jnp.bfloat16)
    outgoing = jnp.dot(
        placing_bf, message.reshape(blocks, block_len * width), preferred_element_type=jnp.float32
    )
    outgoing = outgoing.astype(jnp.bfloat16).reshape(2, CAP, block_len, width)
    out_target = jnp.dot(placing_int, target_grid + 1, preferred_element_type=jnp.int32) - 1
    out_target = out_target.reshape(2, CAP, block_len)
    arriving = padded_2(outgoing, (("lon", 0),), 1)
    arriving_target = padded_2(out_target, (("lon", 0),), 1)
    received = jnp.concatenate([arriving[0], arriving[3]], 0).reshape(-1, width)
    received_target = jnp.concatenate([arriving_target[0], arriving_target[3]], 0).reshape(-1)
    received_safe = jnp.where(received_target < 0, grid_rows, received_target)
    all_target = jnp.concatenate([own_target, received_safe], 0)
    target_hot = jnp.transpose(hot_table(all_target, grid_rows))
    all_message = jnp.concatenate([message, received], 0)
    grid_out = jnp.dot(target_hot, all_message, preferred_element_type=jnp.float32).astype(
        jnp.bfloat16
    )
    all_cot = contract_first(target_hot, grid_cotangent)
    replies = all_cot[own_edges:].astype(jnp.bfloat16).reshape(2, CAP, block_len, width)
    answered = padded_2(replies, (("lon", 0),), 1)
    foreign = jnp.concatenate([answered[0], answered[3]], 0).reshape(2 * CAP, block_len * width)
    foreign_cot = jnp.dot(placing_bf.T, foreign, preferred_element_type=jnp.float32).reshape(
        own_edges, width
    )
    edge_cot = all_cot[:own_edges] + foreign_cot
    d_pre = (edge_cot * silu_slope(pre)).astype(jnp.bfloat16)
    grad_decode = jnp.dot(gathered.T, d_pre, preferred_element_type=jnp.float32)
    per_source = contract_first(source_hot, d_pre).astype(jnp.bfloat16)
    d_out = jnp.dot(per_source, w_decode.T, preferred_element_type=jnp.float32)
    d_node = (d_out * silu_slope(npre)).astype(jnp.bfloat16)
    grad_node = jnp.dot(agg.T, d_node, preferred_element_type=jnp.float32)
    d_coarse = jnp.dot(onehot.T, d_node, preferred_element_type=jnp.float32)
    grad_coarse = jnp.dot(
        coarse_in.astype(jnp.float32).T,
        d_coarse * silu_slope(cpre),
        precision=lax.Precision.HIGHEST,
    )
    d_agg = jnp.dot(d_node, w_node.T, preferred_element_type=jnp.float32)
    d_edges = (d_agg[None] * silu_slope(edges_pre)).astype(jnp.bfloat16)
    grad_source = jnp.dot(
        beside.T, d_edges.reshape(6 * nodes, width), preferred_element_type=jnp.float32
    )
    d_sum = jnp.sum(d_edges.astype(jnp.float32), 0).astype(jnp.bfloat16)
    grad_target = jnp.dot(latent.T, d_sum, preferred_element_type=jnp.float32)
    stacked = jnp.stack([grad_source, grad_target, grad_node, grad_coarse, grad_decode]).reshape(
        5, width * width
    )
    total = lax.psum(stacked, ("lat", "lon"))
    norm = jnp.sqrt(jnp.sum(total * total))
    share_len = width * width // lax.axis_size(("lat", "lon"))
    share = lax.dynamic_slice_in_dim(
        total, lax.axis_index(("lat", "lon")) * share_len, share_len, 1
    )
    clipped = share / (norm + 1e-06)
    return (mesh_out.reshape(height, breadth, width), grid_out, clipped)


def solution(mesh):
    in_specs = (
        P("lat", "lon", None),
        P(("lat", "lon"), None),
        P(),
        P(),
        P(),
        P(),
        P(),
        P(None, "lat", "lon"),
        P("lat", "lon", None),
        P(("lat", "lon")),
        P(("lat", "lon")),
        P(("lat", "lon"), None),
    )
    out_specs = (P("lat", "lon", None), P(("lat", "lon"), None), P(None, ("lat", "lon")))
    return jax.shard_map(local, mesh=mesh, in_specs=in_specs, out_specs=out_specs, check_vma=False)
```

profile of v0, /device:TPU:0, one launch (start us, length us, event | category | flops | bytes accessed | tf_op | source)
XLA Modules:
  0.0 401.5 jit_solution(11711178313239161974)
XLA Ops:
  7.2 0.8 compare_bitcast_fusion
  8.5 0.7 compare_select_fusion.6
  9.2 0.8 convolution_add_fusion.1
  10.1 0.5 collective-permute-start.4
  10.6 2.9 collective-permute-start.5
  13.6 0.7 fusion.62
  14.3 4.3 %collective-permute-start.1 = (bf16[1,8,512]{2,1,0:T(8,128)(2,1)S(1)}, bf16[1,8,512]{2,1,0:T(8,128)(2,1)S(1)}, u32[]{:S(2)}, u32[]{:S(2)}) collective-permute-start(bf16[1,8,512]{2,1,0:T(8,128)(2,1)S(1)} %get-tuple-element.13), channel_id=1, source_target_pairs={{8,0},{16,8},{24,16},{0,24},{9,1},{17,9},{25,17},{1,25},{10,2},{18... | collective-permute-start | bytes 24584 | tf_op jit(solution)/shard_map/ppermute | solution.py:19
  18.6 0.5 broadcast.194
  19.1 1.3 reduce.6
  20.5 2.4 fusion.25
  23.1 0.8 bitcast_select_fusion
  23.9 0.8 fusion.42
  24.7 1.0 fusion.34
  25.9 39.5 %psum.22 = f32[642]{0:T(1024)S(1)} all-reduce(f32[642]{0:T(1024)S(1)} %convert_reduce_fusion), channel_id=1, replica_groups=mesh['lat'=4,'lon'=8] {'lat','lon'}, use_global_device_ids=true, to_apply=%region_3.4 | all-reduce | flops 642 | bytes 5136 | tf_op jit(solution)/shard_map/psum | solution.py:82
  65.5 6.8 %fusion.63 = (bf16[3840,512]{1,0:T(8,128)(2,1)S(1)}, f32[3840,512]{1,0:T(8,128)}) fusion(bf16[1024,512]{1,0:T(8,128)(2,1)S(1)} %copy-done, s32[3840]{0:T(1024)S(1)} %pad_add_fusion), kind=kOutput, calls=%fused_computation.125 | convolution fusion | flops 4032430080 | bytes 12860416 | tf_op jit(solution)/shard_map/dot_general | solution.py:36
  72.5 2.6 collective-permute-start.3
  75.1 1.0 fusion.59
  76.1 0.8 collective-permute-start.9
  77.0 0.3 convolution_convert_fusion.2
  77.4 0.4 fusion.64
  77.8 0.2 multiply_reduce_fusion.1
  78.0 0.2 fusion.67
  78.2 8.5 %collective-permute-done.9 = bf16[1,3,128,512]{3,2,1,0:T(8,128)(2,1)} collective-permute-done((bf16[1,3,128,512]{3,2,1,0:T(8,128)(2,1)}, bf16[1,3,128,512]{3,2,1,0:T(8,128)(2,1)}, u32[]{:S(2)}, u32[]{:S(2)}) %collective-permute-start.9) | collective-permute-done | bytes 393248 | tf_op jit(solution)/shard_map/ppermute | solution.py:19
  86.7 1.3 copy.26
  88.0 0.6 collective-permute-done.8
  88.6 0.3 copy.25
  89.0 3.6 fusion.15
  92.6 7.0 %reshape.162 = f32[3072,512]{1,0:T(8,128)} reshape(f32[24,65536]{1,0:T(8,128)} %fusion.15) | data formatting | bytes 12582912 | tf_op jit(solution)/shard_map/reshape | solution.py:135
  99.6 55.5 %all-reduce.3.cloned.1.call-done = f32[642,512]{1,0:T(8,128)} async-done(((f32[642,512]{1,0:T(8,128)}), f32[642,512]{1,0:T(8,128)}) %all-reduce.3.cloned.1.call-update) | async-done | bytes 1314832 | tf_op jit(solution)/shard_map/psum | solution.py:82
  155.1 1.9 fusion.58
  157.1 0.6 add_convert_fusion
  157.6 0.5 copy-done.7
  158.1 1.7 convolution_convert_fusion.1
  159.9 1.8 fusion.65
  161.7 0.7 slice-done.3
  162.4 0.6 slice-done.1
  163.0 4.7 %fusion.5 = (bf16[3072,512]{1,0:T(8,128)(2,1)S(1)}, bf16[3072,512]{1,0:T(8,128)(2,1)}) fusion(f32[3072,512]{1,0:T(8,128)S(1)} %bitcast.107, f32[3840,512]{1,0:T(8,128)S(1)} %bitcast.111, f32[3072,512]{1,0:T(8,128)S(1)} %fusion.65), kind=kLoop, calls=%fused_computation.9 | loop fusion | flops 18874368 | bytes 25165824 | tf_op jit(solution)/shard_map/convert_element_type | solution.py:139
  167.7 2.8 convolution_bitcast_fusion
  170.5 3.2 fusion.13
  173.7 2.0 convolution_multiply_fusion
  175.7 0.3 fusion.66
  176.0 0.3 fusion.23
  176.3 0.3 fusion.19
  176.7 0.3 convolution_bitcast_fusion.2
  177.1 1.6 convolution_bitcast_fusion.1
  178.7 1.1 copy.30
  179.8 2.1 copy.31
  181.9 0.5 convolution_bitcast_fusion.4
  182.3 2.1 copy.27
  184.4 2.1 copy.29
  186.5 0.3 convolution_bitcast_fusion.3
  186.8 0.3 copy.22
  187.2 1.1 copy.28
  188.2 19.5 %stack.23 = f32[5,262144]{1,0:T(8,128)} concatenate(f32[1,262144]{1,0:T(1,128)} %bitcast.115, f32[1,262144]{1,0:T(1,128)S(1)} %bitcast.117, f32[1,262144]{1,0:T(1,128)} %bitcast.116, f32[1,262144]{1,0:T(1,128)S(1)} %bitcast.113, f32[1,262144]{1,0:T(1,128)} %bitcast.114), dimensions={0} | concatenate | bytes 10485760 | tf_op jit(solution)/shard_map/stack | solution.py:158
  207.8 5.4 %reshape.160 = bf16[24,65536]{1,0:T(8,128)(2,1)} reshape(bf16[3072,512]{1,0:T(8,128)(2,1)} %get-tuple-element.6) | data formatting | bytes 6291456 | tf_op jit(solution)/shard_map/reshape | solution.py:115
  213.2 3.2 convolution_convert_fusion
  216.4 0.4 fusion.60
  216.9 1.1 collective-permute-start.7
  218.0 17.8 %collective-permute-done.7 = bf16[1,3,128,512]{3,2,1,0:T(8,128)(2,1)S(1)} collective-permute-done((bf16[1,3,128,512]{3,2,1,0:T(8,128)(2,1)S(1)}, bf16[1,3,128,512]{3,2,1,0:T(8,128)(2,1)S(1)}, u32[]{:S(2)}, u32[]{:S(2)}) %collective-permute-start.7) | collective-permute-done | bytes 393248 | tf_op jit(solution)/shard_map/ppermute | solution.py:19
  235.8 2.9 collective-permute-done.6
  238.8 7.9 %fusion.10 = bf16[1024,512]{1,0:T(8,128)(2,1)} fusion(bf16[768,512]{1,0:T(8,128)(2,1)S(1)} %bitcast.122, bf16[3072,512]{1,0:T(8,128)(2,1)} %get-tuple-element.6, s32[3840]{0:T(1024)S(1)} %pad_add_fusion), kind=kOutput, calls=%fused_computation.18 | convolution fusion | flops 4038852608 | bytes 4996096 | tf_op jit(solution)/shard_map/dot_general | solution.py:128
  246.7 140.4 %all-reduce.5.cloned.1.call-done = f32[5,262144]{1,0:T(8,128)} async-done(((f32[5,262144]{1,0:T(8,128)}), f32[5,262144]{1,0:T(8,128)}) %all-reduce.5.cloned.1.call-update) | async-done | bytes 5242896 | tf_op jit(solution)/shard_map/psum | solution.py:161
  387.1 5.1 %multiply_reduce_fusion = f32[]{:T(128)} fusion(f32[5,262144]{1,0:T(8,128)} %all-reduce.5.cloned.1.call-done), kind=kLoop, calls=%fused_computation.4 | loop fusion | flops 2621439 | bytes 5242884 | tf_op jit(solution)/shard_map/reduce_sum | solution.py:162
  392.9 1.7 dynamic-slice_divide_fusion
  (87 shorter events, 1.8 us)
Async XLA Ops:
  7.2 58.4 %copy-start = (bf16[1024,512]{1,0:T(8,128)(2,1)S(1)}, bf16[1024,512]{1,0:T(8,128)(2,1)}, u32[]{:S(2)}) copy-start(bf16[1024,512]{1,0:T(8,128)(2,1)} %param.13) | copy-start | bytes 3145732
  7.2 17.5 %copy-start.12 = (bf16[512,512]{1,0:T(8,128)(2,1)S(1)}, bf16[512,512]{1,0:T(8,128)(2,1)}, u32[]{:S(2)}) copy-start(bf16[512,512]{1,0:T(8,128)(2,1)} %param.15) | copy-start | bytes 1572868
  7.2 148.0 %all-reduce.3.cloned.1.call-start = ((), (), s32[]{:S(2)}) async-start(), calls=%async_computation | async-start | bytes 2654208 | tf_op jit(solution)/shard_map/psum | solution.py:82
  9.2 79.8 %copy-start.16 = (s32[24]{0:T(128)}, s32[24]{0:T(128)S(1)}, u32[]{:S(2)}) copy-start(s32[24]{0:T(128)S(1)} %compare_select_fusion.6) | copy-start | bytes 292
  10.1 55.4 %collective-permute-start.4 = (s32[1,3,128]{2,1,0:T(4,128)S(1)}, s32[1,3,128]{2,1,0:T(4,128)S(1)}, u32[]{:S(2)}, u32[]{:S(2)}) collective-permute-start(s32[1,3,128]{2,1,0:T(4,128)S(1)} %get-tuple-element.15), channel_id=1, source_target_pairs={{0,1},{1,2},{2,3},{3,4},{4,5},{5,6},{6,7},{7,0},{8,9},{9,10},{10,1... | collective-permute-start | bytes 4616 | tf_op jit(solution)/shard_map/ppermute | solution.py:17
  10.6 54.9 %collective-permute-start.5 = (s32[1,3,128]{2,1,0:T(4,128)S(1)}, s32[1,3,128]{2,1,0:T(4,128)S(1)}, u32[]{:S(2)}, u32[]{:S(2)}) collective-permute-start(s32[1,3,128]{2,1,0:T(4,128)S(1)} %get-tuple-element.16), channel_id=1, source_target_pairs={{1,0},{2,1},{3,2},{4,3},{5,4},{6,5},{7,6},{0,7},{9,8},{10,9},{11,1... | collective-permute-start | bytes 4616 | tf_op jit(solution)/shard_map/ppermute | solution.py:19
  14.3 58.1 %collective-permute-start.1 = (bf16[1,8,512]{2,1,0:T(8,128)(2,1)S(1)}, bf16[1,8,512]{2,1,0:T(8,128)(2,1)S(1)}, u32[]{:S(2)}, u32[]{:S(2)}) collective-permute-start(bf16[1,8,512]{2,1,0:T(8,128)(2,1)S(1)} %get-tuple-element.13), channel_id=1, source_target_pairs={{8,0},{16,8},{24,16},{0,24},{9,1},{17,9},{25,17},{1,25},{10,2},{18... | collective-permute-start | bytes 24584 | tf_op jit(solution)/shard_map/ppermute | solution.py:19
  18.6 53.8 %collective-permute-start = (bf16[1,8,512]{2,1,0:T(8,128)(2,1)S(1)}, bf16[1,8,512]{2,1,0:T(8,128)(2,1)S(1)}, u32[]{:S(2)}, u32[]{:S(2)}) collective-permute-start(bf16[1,8,512]{2,1,0:T(8,128)(2,1)S(1)} %get-tuple-element.14), channel_id=1, source_target_pairs={{0,8},{8,16},{16,24},{24,0},{1,9},{9,17},{17,25},{25,1},{2,10},{10... | collective-permute-start | bytes 24584 | tf_op jit(solution)/shard_map/ppermute | solution.py:17
  20.5 136.5 %copy-start.18 = (s32[64]{0:T(128)}, s32[64]{0:T(128)S(1)}, u32[]{:S(2)}) copy-start(s32[64]{0:T(128)S(1)} %eq.139) | copy-start | bytes 772
  22.9 364.1 %all-reduce.5.cloned.1.call-start = ((), (), s32[]{:S(2)}) async-start(), calls=%async_computation.1 | async-start | bytes 16777216 | tf_op jit(solution)/shard_map/psum | solution.py:161
  65.5 6.8 %copy-start.8 = (bf16[8,8,512]{2,1,0:T(8,128)(2,1)S(1)}, bf16[8,8,512]{2,1,0:T(8,128)(2,1)}, u32[]{:S(2)}) copy-start(bf16[8,8,512]{2,1,0:T(8,128)(2,1)} %param.12) | copy-start | bytes 196612
  72.4 5.0 %copy-start.13 = (bf16[512,512]{1,0:T(8,128)(2,1)S(1)}, bf16[512,512]{1,0:T(8,128)(2,1)}, u32[]{:S(2)}) copy-start(bf16[512,512]{1,0:T(8,128)(2,1)} %param.14) | copy-start | bytes 1572868
  72.4 5.6 %copy-start.4 = (bf16[512,512]{1,0:T(8,128)(2,1)S(1)}, bf16[512,512]{1,0:T(8,128)(2,1)}, u32[]{:S(2)}) copy-start(bf16[512,512]{1,0:T(8,128)(2,1)} %param.16) | copy-start | bytes 1572868
  72.5 4.5 %collective-permute-start.2 = (bf16[10,1,512]{2,1,0:T(2,128)(2,1)S(1)}, bf16[10,1,512]{2,1,0:T(2,128)(2,1)S(1)}, u32[]{:S(2)}, u32[]{:S(2)}) collective-permute-start(bf16[10,1,512]{2,1,0:T(2,128)(2,1)S(1)} %get-tuple-element.11), channel_id=1, source_target_pairs={{0,1},{1,2},{2,3},{3,4},{4,5},{5,6},{6,7},{7,0},{8,9},{9,10},{10,1... | collective-permute-start | bytes 30728 | tf_op jit(solution)/shard_map/ppermute | solution.py:17
  72.5 4.4 %collective-permute-start.3 = (bf16[10,1,512]{2,1,0:T(2,128)(2,1)S(1)}, bf16[10,1,512]{2,1,0:T(2,128)(2,1)S(1)}, u32[]{:S(2)}, u32[]{:S(2)}) collective-permute-start(bf16[10,1,512]{2,1,0:T(2,128)(2,1)S(1)} %get-tuple-element.12), channel_id=1, source_target_pairs={{1,0},{2,1},{3,2},{4,3},{5,4},{6,5},{7,6},{0,7},{9,8},{10,9},{11,1... | collective-permute-start | bytes 30728 | tf_op jit(solution)/shard_map/ppermute | solution.py:19
  76.1 10.5 %collective-permute-start.9 = (bf16[1,3,128,512]{3,2,1,0:T(8,128)(2,1)}, bf16[1,3,128,512]{3,2,1,0:T(8,128)(2,1)}, u32[]{:S(2)}, u32[]{:S(2)}) collective-permute-start(bf16[1,3,128,512]{3,2,1,0:T(8,128)(2,1)} %bitcast.16), channel_id=1, source_target_pairs={{1,0},{2,1},{3,2},{4,3},{5,4},{6,5},{7,6},{0,7},{9,8},{10,9},{11,1... | collective-permute-start | bytes 1179656 | tf_op jit(solution)/shard_map/ppermute | solution.py:19
  76.9 11.7 %collective-permute-start.8 = (bf16[1,3,128,512]{3,2,1,0:T(8,128)(2,1)}, bf16[1,3,128,512]{3,2,1,0:T(8,128)(2,1)S(1)}, u32[]{:S(2)}, u32[]{:S(2)}) collective-permute-start(bf16[1,3,128,512]{3,2,1,0:T(8,128)(2,1)} %bitcast.15), channel_id=1, source_target_pairs={{0,1},{1,2},{2,3},{3,4},{4,5},{5,6},{6,7},{7,0},{8,9},{9,10},{10,1... | collective-permute-start | bytes 1179656 | tf_op jit(solution)/shard_map/ppermute | solution.py:17
  92.6 62.5 %copy-start.11 = (bf16[512,512]{1,0:T(8,128)(2,1)S(1)}, bf16[512,512]{1,0:T(8,128)(2,1)}, u32[]{:S(2)}) copy-start(bf16[512,512]{1,0:T(8,128)(2,1)} %param.17) | copy-start | bytes 1572868
  157.0 1.1 copy-start.7
  157.0 1.1 copy-start.14
  157.1 4.6 %slice-start.2 = ((s8[7864320]{0:T(1024)(128)(4,1)}), s8[4194304]{0:T(1024)(128)(4,1)S(1)}, s32[]{:S(2)}) async-start(s8[7864320]{0:T(1024)(128)(4,1)} %bitcast.110), calls=%async_computation.4 | async-start | bytes 8388608
  158.1 3.5 copy-start.15
  158.1 1.8 copy-start.5
  158.1 3.6 slice-start
  158.1 4.2 %slice-start.3 = ((s8[7864320]{0:T(1024)(128)(4,1)}), s8[3670016]{0:T(1024)(128)(4,1)S(1)}, s32[]{:S(2)}) async-start(s8[7864320]{0:T(1024)(128)(4,1)} %bitcast.110), calls=%async_computation.5 | async-start | bytes 7340032
  159.9 3.1 slice-start.1
  167.7 2.8 copy-start.2
  167.7 2.8 copy-start.6
  170.5 3.2 copy-start.19
  175.7 1.3 copy-start.3
  177.1 2.7 copy-start.10
  181.9 4.6 %copy-start.9 = (bf16[8,8,512]{2,1,0:T(8,128)(2,1)S(1)}, bf16[8,8,512]{2,1,0:T(8,128)(2,1)}, u32[]{:S(2)}) copy-start(bf16[8,8,512]{2,1,0:T(8,128)(2,1)} %param.12) | copy-start | bytes 196612
  207.8 5.5 %copy-start.17 = (s32[24]{0:T(128)S(1)}, s32[24]{0:T(128)}, u32[]{:S(2)}) copy-start(s32[24]{0:T(128)} %copy-done.16) | copy-start | bytes 292
  216.9 18.9 %collective-permute-start.7 = (bf16[1,3,128,512]{3,2,1,0:T(8,128)(2,1)S(1)}, bf16[1,3,128,512]{3,2,1,0:T(8,128)(2,1)S(1)}, u32[]{:S(2)}, u32[]{:S(2)}) collective-permute-start(bf16[1,3,128,512]{3,2,1,0:T(8,128)(2,1)S(1)} %copy.34), channel_id=1, source_target_pairs={{1,0},{2,1},{3,2},{4,3},{5,4},{6,5},{7,6},{0,7},{9,8},{10,9},{11,1... | collective-permute-start | bytes 1179656 | tf_op jit(solution)/shard_map/ppermute | solution.py:19
  218.0 20.7 %collective-permute-start.6 = (bf16[1,3,128,512]{3,2,1,0:T(8,128)(2,1)S(1)}, bf16[1,3,128,512]{3,2,1,0:T(8,128)(2,1)S(1)}, u32[]{:S(2)}, u32[]{:S(2)}) collective-permute-start(bf16[1,3,128,512]{3,2,1,0:T(8,128)(2,1)S(1)} %copy.35), channel_id=1, source_target_pairs={{0,1},{1,2},{2,3},{3,4},{4,5},{5,6},{6,7},{7,0},{8,9},{9,10},{10,1... | collective-permute-start | bytes 1179656 | tf_op jit(solution)/shard_map/ppermute | solution.py:17
  238.8 155.8 %copy-start.1 = (bf16[1024,512]{1,0:T(8,128)(2,1)S(1)}, bf16[1024,512]{1,0:T(8,128)(2,1)}, u32[]{:S(2)}) copy-start(bf16[1024,512]{1,0:T(8,128)(2,1)} %param.13) | copy-start | bytes 3145732
Sparse Core Ops, SparseCore 0:
  23.1 132.0 all-reduce.2
  207.9 179.1 all-reduce.4
where the time goes:
time: 404 us; the launch traced here: 401 us
  waiting for transfers between devices  226 us (56%)
  local copies, waits for them, and re-layouts  47.7 us (12%)
  matrix products  43.5 us (11%)
  blocking collectives  39.5 us (10%)
  other arithmetic  17.4 us (4%)
  between operations  15.2 us (4%)
  starting transfers between devices  12.4 us (3%)
    psum x1, waiting for transfers between devices, local(): total = lax.psum(stacked, ('lat', 'lon'))  140 us
    psum x1, waiting for transfers between devices, local(): pooled, count = lax.psum((pooled_part, count_part), ('lat', 'lon'))  55.5 us
    psum x1, blocking collectives, local(): pooled, count = lax.psum((pooled_part, count_part), ('lat', 'lon'))  39.5 us
    ppermute x5, waiting for transfers between devices, padded_2(): lax.ppermute(head, axis, [((i + 1) % count, i) for i in range(count)])  26.2 us
    another operation x1, local copies, waits for them, and re-layouts, local(): jnp.stack([grad_source, grad_target, grad_node, grad_coarse, grad_decode])  19.5 us
    unnamed x60, local copies, waits for them, and re-layouts  12.8 us
    ppermute x5, starting transfers between devices, padded_2(): lax.ppermute(head, axis, [((i + 1) % count, i) for i in range(count)])  11.7 us
  transfers between devices with their start and end apart: 12, of which 6 were waited for; matrix products, arithmetic and copies ran while one was open for 12% of the time, Pallas kernels for 0%

commit v1 on v0

v1 whole, which is shorter than its diff:
```python
import jax
import jax.numpy as jnp
from jax import lax
from jax.sharding import PartitionSpec as P

CAP = 3
AXES = ("lat", "lon")
F32 = jnp.float32
BF16 = jnp.bfloat16


def silu_slope(value):
    sig = jax.nn.sigmoid(value)
    return sig * (1.0 + value * (1.0 - sig))


def mm(left, right):
    return jnp.dot(left, right, preferred_element_type=F32)


def mm_t(left, right):
    return lax.dot_general(left, right, (((0,), (0,)), ((), ())), preferred_element_type=F32)


def mm_nt(left, right):
    return lax.dot_general(left, right, (((1,), (1,)), ((), ())), preferred_element_type=F32)


def split_counts(counts):
    high = jnp.floor(counts * (1.0 / 256.0)) * 256.0
    return high.astype(BF16), (counts - high).astype(BF16)


def split_float(value):
    high = value.astype(BF16)
    return high, (value - high.astype(F32)).astype(BF16)


def shift(value, axis, step):
    count = lax.axis_size(axis)
    return lax.ppermute(value, axis, [(i, (i + step) % count) for i in range(count)])


def packed_edges(edge_source, edge_target, edge_owner, grid_rows, nodes):
    lon_pos = lax.axis_index("lon")
    lon_count = lax.axis_size("lon")
    blocks = edge_owner.shape[0]
    block_len = edge_source.shape[0] // blocks
    side = (edge_owner[:, 0] - lon_pos + lon_count) % lon_count
    to_left = (side == lon_count - 1).astype(jnp.int32)
    to_right = (side == 1).astype(jnp.int32)
    tri = (jnp.arange(blocks)[:, None] > jnp.arange(blocks)[None, :]).astype(jnp.int32)
    left_rank = jnp.sum(tri * to_left[None, :], 1)
    right_rank = jnp.sum(tri * to_right[None, :], 1)
    place = jnp.where(to_left == 1, left_rank, jnp.where(to_right == 1, CAP + right_rank, -1))
    placing = jnp.arange(2 * CAP, dtype=jnp.int32)[:, None] == place[None, :]
    sources = edge_source.reshape(blocks, block_len)
    targets = edge_target.reshape(blocks, block_len)
    code = sources * (grid_rows + 1) + targets + 1
    packed = jnp.sum(jnp.where(placing[:, :, None], code[None], 0), 1).reshape(2, CAP * block_len)
    own_target = jnp.where((side == 0)[:, None], targets, -1).reshape(-1)
    return own_target, packed


def local(
    mesh_latent,
    grid_cotangent,
    w_source,
    w_target,
    w_node,
    w_coarse,
    w_decode,
    neighbour_codes,
    coarse_ids,
    edge_source,
    edge_target,
    edge_owner,
):
    height, breadth, width = mesh_latent.shape
    nodes = height * breadth
    grid_rows = grid_cotangent.shape[0]
    lat_pos, lon_pos = lax.axis_index("lat"), lax.axis_index("lon")
    lat_count, lon_count = lax.axis_size("lat"), lax.axis_size("lon")
    latent = mesh_latent.reshape(nodes, width)
    ids = coarse_ids.reshape(nodes)
    everyone = lax.all_gather(latent, AXES, axis=0, tiled=True)
    all_ids = lax.all_gather(ids, AXES, axis=0, tiled=True)

    own_target, packed = packed_edges(edge_source, edge_target, edge_owner, grid_rows, nodes)
    from_right = shift(packed[0], "lon", -1)
    from_left = shift(packed[1], "lon", 1)
    foreign = jnp.concatenate([from_left, from_right])
    offsets = jnp.repeat(jnp.array([1, 2], jnp.int32) * nodes, from_left.shape[0])
    every_target = jnp.concatenate([own_target, foreign % (grid_rows + 1) - 1])
    every_source = jnp.concatenate([edge_source, foreign // (grid_rows + 1) + offsets])
    target_hot = (jnp.arange(grid_rows, dtype=jnp.int32)[:, None] == every_target[None]).astype(BF16)
    source_hot = (every_source[:, None] == jnp.arange(3 * nodes, dtype=jnp.int32)[None]).astype(BF16)
    counts = mm(target_hot, source_hot)
    count_high, count_low = split_counts(counts)
    cot_sums = mm_t(count_high, grid_cotangent) + mm_t(count_low, grid_cotangent)
    back = cot_sums[nodes:].astype(BF16)
    cot_sum = (
        cot_sums[:nodes]
        + shift(back[:nodes], "lon", -1).astype(F32)
        + shift(back[nodes:], "lon", 1).astype(F32)
    )

    rows = lat_pos * height + jnp.arange(height, dtype=jnp.int32)[None, :, None] + neighbour_codes // 3 - 1
    cols = lon_pos * breadth + jnp.arange(breadth, dtype=jnp.int32)[None, None, :] + neighbour_codes % 3 - 1
    inside = (rows >= 0) & (rows < lat_count * height)
    cols = (cols + lon_count * breadth) % (lon_count * breadth)
    where_idx = ((rows // height) * lon_count + cols // breadth) * nodes + (rows % height) * breadth + cols % breadth
    where_idx = jnp.where(inside, where_idx, -1).reshape(-1)
    positions = jnp.arange(everyone.shape[0], dtype=jnp.int32)
    beside = mm((where_idx[:, None] == positions[None]).astype(BF16), everyone).astype(BF16)
    toward = mm(latent, w_target)
    edges_pre = mm(beside, w_source).reshape(6, nodes, width) + toward[None]
    agg = jnp.sum(jax.nn.silu(edges_pre), 0).astype(BF16)

    same = (ids[:, None] == all_ids[None]).astype(BF16)
    pooled = mm(same, everyone)
    count = jnp.sum(same.astype(F32), 1)
    coarse_in = (pooled * lax.rsqrt(count)[:, None]).astype(BF16)
    cpre = mm(coarse_in, w_coarse)
    coarse_out = jax.nn.silu(cpre).astype(BF16)
    npre = mm(agg, w_node) + coarse_out.astype(F32)
    mesh_out = (latent.astype(F32) + jax.nn.silu(npre)).astype(BF16)

    pre = mm(mesh_out, w_decode)
    message = jax.nn.silu(pre).astype(BF16)
    messages = jnp.concatenate([message, shift(message, "lon", 1), shift(message, "lon", -1)], 0)
    grid_out = (mm(count_high, messages) + mm(count_low, messages)).astype(BF16)

    d_pre = cot_sum * silu_slope(pre)
    d_high, d_low = split_float(d_pre)
    grad_decode = mm_t(mesh_out, d_high) + mm_t(mesh_out, d_low)
    d_out = mm_nt(d_high, w_decode)
    d_node = (d_out * silu_slope(npre)).astype(BF16)
    grad_node = mm_t(agg, d_node)
    c_high, c_low = split_float(d_node.astype(F32) * silu_slope(cpre))
    grad_coarse = mm_t(coarse_in, c_high) + mm_t(coarse_in, c_low)
    d_agg = mm_nt(d_node, w_node)
    d_edges = (d_agg[None] * silu_slope(edges_pre)).astype(BF16)
    grad_source = mm_t(beside, d_edges.reshape(6 * nodes, width))
    d_sum = jnp.sum(d_edges.astype(F32), 0).astype(BF16)
    grad_target = mm_t(latent, d_sum)
    stacked = jnp.stack([grad_source, grad_target, grad_node, grad_coarse, grad_decode]).reshape(
        5, width * width
    )
    share = lax.psum_scatter(stacked, AXES, scatter_dimension=1, tiled=True)
    norm = jnp.sqrt(lax.psum(jnp.sum(share * share), AXES))
    clipped = share / (norm + 1e-06)
    return (mesh_out.reshape(height, breadth, width), grid_out, clipped)


def solution(mesh):
    in_specs = (
        P("lat", "lon", None),
        P(("lat", "lon"), None),
        P(),
        P(),
        P(),
        P(),
        P(),
        P(None, "lat", "lon"),
        P("lat", "lon", None),
        P(("lat", "lon")),
        P(("lat", "lon")),
        P(("lat", "lon"), None),
    )
    out_specs = (P("lat", "lon", None), P(("lat", "lon"), None), P(None, ("lat", "lon")))
    return jax.shard_map(local, mesh=mesh, in_specs=in_specs, out_specs=out_specs, check_vma=False)
```

time: 404 us -> 317 us (0.78)
  waiting for transfers between devices: 226 us -> 149 us
  blocking collectives: 39.5 us -> 77.4 us
  matrix products: 43.5 us -> 19 us
  local copies, waits for them, and re-layouts: 47.7 us -> 37.1 us
  other arithmetic: 17.4 us -> 8.73 us
  starting transfers between devices: 12.4 us -> 7.22 us
    psum x2 -> x0, waiting for transfers between devices: 196 us -> none  [the longest x1 140 us: local(): total = lax.psum(stacked, ('lat', 'lon'))]
    reduce_scatter x0 -> x1, waiting for transfers between devices: none -> 143 us  [local(): share = lax.psum_scatter(stacked, AXES, scatter_dimension=1, tiled=True)]
    unnamed x0 -> x1, blocking collectives: none -> 40.4 us
    ppermute x10 -> x6, waiting for transfers between devices: 29.8 us -> 1.96 us  [shift(): lax.ppermute(value, axis, [(i, (i + step) % count) for i in range(count)])]
    dot_general x22 -> x21, matrix products: 43.5 us -> 19 us  [the longest x10 14.4 us: mm(): return jnp.dot(left, right, preferred_element_type=F32)]
    reshape x2 -> x1, local copies, waits for them, and re-layouts: 12.4 us -> 0.01 us  [local(): jnp.repeat(jnp.array([1, 2], jnp.int32) * nodes, from_left.shape[0])]
    ppermute x10 -> x6, starting transfers between devices: 12.3 us -> 7.14 us  [shift(): lax.ppermute(value, axis, [(i, (i + step) % count) for i in range(count)])]
    unnamed x60 -> x31, local copies, waits for them, and re-layouts: 12.8 us -> 13.6 us
  transfers between devices with their start and end apart: 12 -> 8, of which waited for: 6 -> 3; matrix products, arithmetic and copies ran while one was open for 12% -> 6% of each run, Pallas kernels for 0% -> 0%
where the time goes in v1:
time: 317 us; the launch traced here: 314 us
  waiting for transfers between devices  149 us (47%)
  blocking collectives  77.4 us (24%)
  local copies, waits for them, and re-layouts  37.1 us (12%)
  matrix products  19 us (6%)
  between operations  15.1 us (5%)
  other arithmetic  8.73 us (3%)
  starting transfers between devices  7.22 us (2%)
    reduce_scatter x1, waiting for transfers between devices, local(): share = lax.psum_scatter(stacked, AXES, scatter_dimension=1, tiled=True)  143 us
    unnamed x1, blocking collectives  40.4 us
    psum x1, blocking collectives, local(): norm = jnp.sqrt(lax.psum(jnp.sum(share * share), AXES))  37 us
    another operation x1, local copies, waits for them, and re-layouts, local(): jnp.stack([grad_source, grad_target, grad_node, grad_coarse, grad_decode])  20 us
    dot_general x10, matrix products, mm(): return jnp.dot(left, right, preferred_element_type=F32)  14.4 us
    unnamed x31, local copies, waits for them, and re-layouts  13.6 us
    ppermute x6, starting transfers between devices, shift(): lax.ppermute(value, axis, [(i, (i + step) % count) for i in range(count)])  7.14 us
  transfers between devices with their start and end apart: 8, of which 3 were waited for; matrix products, arithmetic and copies ran while one was open for 6% of the time, Pallas kernels for 0%

profile of v1, /device:TPU:0, one launch (start us, length us, event | category | flops | bytes accessed | tf_op | source)
XLA Modules:
  0.0 313.7 jit_solution(13218511887426768028)
XLA Ops:
  7.2 0.0 copy-start
  7.2 0.0 all-gather.2.cloned.1.call-start
  7.2 0.7 all-gather.2.cloned.1.call-update
  7.9 0.0 reduce-scatter.2.cloned.1.call-start
  8.0 0.7 compare_convert_fusion.1
  8.6 0.1 select_reduce_fusion.1
  8.8 0.7 compare_bitcast_fusion
  9.4 0.8 bitcast_select_fusion
  10.2 0.1 select_reduce_fusion
  10.4 0.5 collective-permute-start
  10.9 2.9 collective-permute-start.1
  13.8 0.5 broadcast.264
  14.4 1.3 reduce.4
  15.7 0.1 reshape.141
  15.8 0.3 dynamic-update-slice
  16.0 40.4 %all-reduce = s32[2048]{0:T(1024)S(1)} all-reduce(s32[2048]{0:T(1024)S(1)} %dynamic-update-slice), channel_id=1, replica_groups=mesh['lat'=4,'lon'=8] {'lat','lon'}, use_global_device_ids=true, to_apply=%add | all-reduce | flops 2048 | bytes 16384
  56.5 0.8 fusion.35
  57.3 1.3 fusion.57
  58.6 0.2 convert_reduce_fusion
  58.8 0.7 broadcast_in_dim.73
  59.6 0.1 eq.120
  59.7 0.7 pad_add_fusion.1
  60.5 3.9 %fusion = f32[1024,192]{0,1:T(8,128)S(1)} fusion(s32[3840]{0:T(1024)S(1)} %pad_add_fusion, s32[3840]{0:T(1024)S(1)} %pad_add_fusion.1), kind=kOutput, calls=%fused_computation.1 | convolution fusion | flops 1514618880 | bytes 817152 | tf_op jit(solution)/shard_map/dot_general | solution.py:18
  64.4 0.4 fusion.20
  64.8 0.4 fusion.71
  65.2 1.0 collective-permute-start.4
  66.2 3.7 %all-gather.2.cloned.1.call-done = bf16[2048,512]{1,0:T(8,128)(2,1)} async-done(((bf16[64,512]{1,0:T(8,128)(2,1)}), bf16[2048,512]{1,0:T(8,128)(2,1)}) %all-gather.2.cloned.1.call-update) | async-done | bytes 2097168 | tf_op jit(solution)/shard_map/all_gather | solution.py:86
  69.9 2.6 fusion.7
  72.5 0.4 fusion.72
  72.9 0.2 multiply_reduce_fusion
  73.1 1.1 copy-done.1
  74.2 0.5 fusion.8
  74.8 0.2 fusion.73
  75.0 0.2 add_convert_fusion.1
  75.3 0.0 copy-done.10
  75.3 0.3 fusion.17
  75.6 0.3 fusion.19
  75.9 0.3 fusion.9
  76.2 0.3 fusion.24
  76.5 0.3 fusion.74
  76.8 0.3 fusion.13
  77.1 0.3 fusion.10
  77.5 0.3 convolution_bitcast_fusion
  77.8 0.3 fusion.6
  78.1 2.1 copy.21
  80.3 0.3 fusion.5
  80.6 2.0 copy.22
  82.6 1.3 convolution_bitcast_fusion.1
  83.9 2.5 copy.17
  86.5 3.3 %copy.19 = f32[1,1,512,512]{3,1,2,0:T(1,128)} copy(f32[1,1,512,512]{3,2,1,0:T(8,128)} %bitcast.78) | data formatting | bytes 2097152
  89.8 0.5 convolution_bitcast_fusion.2
  90.3 2.1 copy.18
  92.3 2.1 copy.20
  94.4 20.0 %stack.23 = f32[5,262144]{1,0:T(8,128)} concatenate(f32[1,262144]{1,0:T(1,128)} %bitcast.82, f32[1,262144]{1,0:T(1,128)} %bitcast.81, f32[1,262144]{1,0:T(1,128)} %bitcast.83, f32[1,262144]{1,0:T(1,128)} %bitcast.79, f32[1,262144]{1,0:T(1,128)} %bitcast.80), dimensions={0} | concatenate | bytes 10485760 | tf_op jit(solution)/shard_map/stack | solution.py:147
  114.4 0.0 reduce-scatter.2.cloned.1.call-update
  114.4 0.3 collective-permute-start.2
  114.7 2.4 collective-permute-start.3
  117.1 1.9 collective-permute-done.2
  119.1 1.9 fusion.18
  121.0 142.8 %reduce-scatter.2.cloned.1.call-done = f32[5,8192]{1,0:T(8,128)} async-done(((f32[5,262144]{1,0:T(8,128)}), f32[5,8192]{1,0:T(8,128)}) %reduce-scatter.2.cloned.1.call-update) | async-done | bytes 163856 | tf_op jit(solution)/shard_map/reduce_scatter | solution.py:150
  263.8 1.6 multiply_reduce_fusion.1
  265.4 3.1 add_convert_fusion
  268.5 37.0 %psum.7 = f32[]{:T(128)} all-reduce(f32[]{:T(128)} %multiply_reduce_fusion.1), channel_id=1, replica_groups=mesh['lat'=4,'lon'=8] {'lat','lon'}, use_global_device_ids=true, to_apply=%region_8.9 | all-reduce | flops 1 | bytes 8 | tf_op jit(solution)/shard_map/psum | solution.py:151
  306.2 0.7 broadcast_divide_fusion
  (39 shorter events, 0.1 us)
Async XLA Ops:
  7.2 57.2 %copy-start = (bf16[1024,512]{1,0:T(8,128)(2,1)S(1)}, bf16[1024,512]{1,0:T(8,128)(2,1)}, u32[]{:S(2)}) copy-start(bf16[1024,512]{1,0:T(8,128)(2,1)} %param.14) | copy-start | bytes 3145732
  7.2 62.7 %all-gather.2.cloned.1.call-start = ((), (), s32[]{:S(2)}) async-start(), calls=%async_computation.1 | async-start | bytes 2162688 | tf_op jit(solution)/shard_map/all_gather | solution.py:86
  7.9 255.8 %reduce-scatter.2.cloned.1.call-start = ((), (), s32[]{:S(2)}) async-start(), calls=%async_computation.2 | async-start | bytes 8650752 | tf_op jit(solution)/shard_map/reduce_scatter | solution.py:150
  10.4 49.3 %collective-permute-start = (s32[384]{0:T(512)S(1)}, s32[384]{0:T(512)S(1)}, u32[]{:S(2)}, u32[]{:S(2)}) collective-permute-start(s32[384]{0:T(512)S(1)} %get-tuple-element.14), channel_id=1, source_target_pairs={{0,1},{1,2},{2,3},{3,4},{4,5},{5,6},{6,7},{7,0},{8,9},{9,10},{10,1... | collective-permute-start | bytes 4616 | tf_op jit(solution)/shard_map/ppermute | solution.py:41
  10.9 48.8 %collective-permute-start.1 = (s32[384]{0:T(512)S(1)}, s32[384]{0:T(512)S(1)}, u32[]{:S(2)}, u32[]{:S(2)}) collective-permute-start(s32[384]{0:T(512)S(1)} %get-tuple-element.13), channel_id=1, source_target_pairs={{0,7},{1,0},{2,1},{3,2},{4,3},{5,4},{6,5},{7,6},{8,15},{9,8},{10,9... | collective-permute-start | bytes 4616 | tf_op jit(solution)/shard_map/ppermute | solution.py:41
  65.2 10.1 %collective-permute-start.4 = (bf16[64,512]{1,0:T(8,128)(2,1)S(1)}, bf16[64,512]{1,0:T(8,128)(2,1)S(1)}, u32[]{:S(2)}, u32[]{:S(2)}) collective-permute-start(bf16[64,512]{1,0:T(8,128)(2,1)S(1)} %get-tuple-element.5), channel_id=1, source_target_pairs={{0,7},{1,0},{2,1},{3,2},{4,3},{5,4},{6,5},{7,6},{8,15},{9,8},{10,9... | collective-permute-start | bytes 196616 | tf_op jit(solution)/shard_map/ppermute | solution.py:41
  66.2 6.3 %copy-start.6 = (bf16[512,512]{1,0:T(8,128)(2,1)S(1)}, bf16[512,512]{1,0:T(8,128)(2,1)}, u32[]{:S(2)}) copy-start(bf16[512,512]{1,0:T(8,128)(2,1)} %param.15) | copy-start | bytes 1572868
  66.2 9.1 %collective-permute-start.5 = (bf16[64,512]{1,0:T(8,128)(2,1)S(1)}, bf16[64,512]{1,0:T(8,128)(2,1)S(1)}, u32[]{:S(2)}, u32[]{:S(2)}) collective-permute-start(bf16[64,512]{1,0:T(8,128)(2,1)S(1)} %get-tuple-element.6), channel_id=1, source_target_pairs={{0,1},{1,2},{2,3},{3,4},{4,5},{5,6},{6,7},{7,0},{8,9},{9,10},{10,1... | collective-permute-start | bytes 196616 | tf_op jit(solution)/shard_map/ppermute | solution.py:41
  72.5 2.3 copy-start.2
  72.5 1.7 copy-start.1
  72.5 2.3 copy-start.7
  72.9 2.1 copy-start.5
  72.9 2.1 copy-start.8
  74.2 1.1 copy-start.10
  75.2 5.0 %copy-start.9 = (bf16[64,512]{1,0:T(8,128)(2,1)}, bf16[64,512]{1,0:T(8,128)(2,1)S(1)}, u32[]{:S(2)}) copy-start(bf16[64,512]{1,0:T(8,128)(2,1)S(1)} %get-tuple-element.15) | copy-start | bytes 196612
  86.5 3.3 %copy-start.3 = (bf16[384,512]{1,0:T(8,128)(2,1)S(1)}, bf16[384,512]{1,0:T(8,128)(2,1)}, u32[]{:S(2)}) copy-start(bf16[384,512]{1,0:T(8,128)(2,1)} %copy-done.2) | copy-start | bytes 1179652
  114.4 4.6 %collective-permute-start.2 = (bf16[64,512]{1,0:T(8,128)(2,1)S(1)}, bf16[64,512]{1,0:T(8,128)(2,1)S(1)}, u32[]{:S(2)}, u32[]{:S(2)}) collective-permute-start(bf16[64,512]{1,0:T(8,128)(2,1)S(1)} %get-tuple-element.8), channel_id=1, source_target_pairs={{0,1},{1,2},{2,3},{3,4},{4,5},{5,6},{6,7},{7,0},{8,9},{9,10},{10,1... | collective-permute-start | bytes 196616 | tf_op jit(solution)/shard_map/ppermute | solution.py:41
  114.7 4.4 %collective-permute-start.3 = (bf16[64,512]{1,0:T(8,128)(2,1)S(1)}, bf16[64,512]{1,0:T(8,128)(2,1)S(1)}, u32[]{:S(2)}, u32[]{:S(2)}) collective-permute-start(bf16[64,512]{1,0:T(8,128)(2,1)S(1)} %get-tuple-element.8), channel_id=1, source_target_pairs={{0,7},{1,0},{2,1},{3,2},{4,3},{5,4},{6,5},{7,6},{8,15},{9,8},{10,9... | collective-permute-start | bytes 196616 | tf_op jit(solution)/shard_map/ppermute | solution.py:41
  265.4 40.8 %copy-start.4 = (f32[5,8192]{1,0:T(8,128)S(1)}, f32[5,8192]{1,0:T(8,128)}, u32[]{:S(2)}) copy-start(f32[5,8192]{1,0:T(8,128)} %reduce-scatter.2.cloned.1.call-done) | copy-start | bytes 491524
Sparse Core Ops, SparseCore 0:
  10.8 58.9 all-gather.1
  114.5 149.1 reduce-scatter.1

commit v2 on v1

--- a/solution.py
+++ b/solution.py
@@ -1,10 +1,14 @@
+import functools
+import math
+
 import jax
 import jax.numpy as jnp
 from jax import lax
+from jax.experimental import pallas as pl
+from jax.experimental.pallas import tpu as pltpu
 from jax.sharding import PartitionSpec as P
 
 CAP = 3
-AXES = ("lat", "lon")
 F32 = jnp.float32
 BF16 = jnp.bfloat16
 
@@ -60,6 +64,302 @@
     packed = jnp.sum(jnp.where(placing[:, :, None], code[None], 0), 1).reshape(2, CAP * block_len)
     own_target = jnp.where((side == 0)[:, None], targets, -1).reshape(-1)
     return own_target, packed
+
+
+MESH = pl.DeviceIdType.MESH
+
+
+class Place:
+    def __init__(self, sizes):
+        self.Z, self.Y, self.X, self.C = sizes
+        self.L = self.Y * self.X * self.C
+        self.lat, self.lon = lax.axis_index("lat"), lax.axis_index("lon")
+        self.z, self.c = self.lat, lax.rem(self.lon, self.C)
+        self.x = lax.rem(self.lon // self.C, self.X)
+        self.y = self.lon // (self.C * self.X)
+
+    def at(self, y=None, x=None, c=None):
+        y, x, c = (old if new is None else new for new, old in ((y, self.y), (x, self.x), (c, self.c)))
+        return (self.lat, (y * self.X + x) * self.C + c)
+
+    def meet(self):
+        barrier = pltpu.get_barrier_semaphore()
+        for step in range(1, self.Z):
+            peer = (lax.rem(self.z + step, self.Z), self.lon)
+            pl.semaphore_signal(barrier, inc=1, device_id=peer, device_id_type=MESH)
+        for step in range(1, self.L):
+            peer = (self.lat, lax.rem(self.lon + step, self.L))
+            pl.semaphore_signal(barrier, inc=1, device_id=peer, device_id_type=MESH)
+        pl.semaphore_wait(barrier, self.Z - 1 + self.L - 1)
+
+
+def send(src, dst, sems, slot, peer):
+    copy = pltpu.make_async_remote_copy(
+        src_ref=src, dst_ref=dst, send_sem=sems.at[0, slot], recv_sem=sems.at[1, slot],
+        device_id=peer, device_id_type=MESH,
+    )
+    copy.start()
+    return copy
+
+
+def gather_kernel(sizes, lat_ref, id_ref, edge_ref, all_ref, all_id_ref, left_ref, right_ref, sems):
+    p = Place(sizes)
+    Z, Y, X, C, z, y, x, c = p.Z, p.Y, p.X, p.C, p.z, p.y, p.x, p.c
+    half = lat_ref.shape[0] // 2
+    low, high = pl.ds(0, half), pl.ds(half, half)
+    used = [0]
+    copies = []
+
+    def go(src, dst, peer):
+        copy = send(src, dst, sems, used[0], peer)
+        used[0] += 1
+        copies.append(copy)
+        return copy
+
+    all_ref[z, y, x, c] = lat_ref[...]
+    all_id_ref[z, y, x, c] = id_ref[...]
+    p.meet()
+    first = []
+    for step in range(1, Z):
+        peer = (lax.rem(z + step, Z), p.lon)
+        first.append([
+            go(lat_ref, all_ref.at[z, y, x, c], peer),
+            go(id_ref, all_id_ref.at[z, y, x, c], peer),
+        ])
+    edges = [
+        go(edge_ref.at[0], right_ref, (p.lat, lax.rem(p.lon + p.L - 1, p.L))),
+        go(edge_ref.at[1], left_ref, (p.lat, lax.rem(p.lon + 1, p.L))),
+    ]
+    second = []
+    for step in range(Z):
+        line = lax.rem(z + Z - step, Z)
+        if step:
+            for copy in first[step - 1]:
+                copy.wait_recv()
+        mine = []
+        block = all_ref.at[line, y, x, c]
+        src_low = block.at[low] if step else lat_ref.at[low]
+        src_high = block.at[high] if step else lat_ref.at[high]
+        src_id = all_id_ref.at[line, y, x, c] if step else id_ref
+        for off in range(1, X):
+            peer = p.at(x=lax.rem(x + off, X))
+            mine.append(go(src_low, block.at[low], peer))
+            mine.append(go(src_id, all_id_ref.at[line, y, x, c], peer))
+        for off in range(1, Y):
+            mine.append(go(src_high, block.at[high], p.at(y=lax.rem(y + off, Y))))
+        second.append(mine)
+    third = []
+    for step in range(Z):
+        line = lax.rem(z + Z - step, Z)
+        for copy in second[step]:
+            copy.wait_recv()
+        mine = []
+        for off in range(1, Y):
+            peer = p.at(y=lax.rem(y + off, Y))
+            part = all_ref.at[line, y, :, c, low]
+            mine.append(go(part, part, peer))
+            part = all_id_ref.at[line, y, :, c]
+            mine.append(go(part, part, peer))
+        for off in range(1, X):
+            part = all_ref.at[line, :, x, c, high]
+            mine.append(go(part, part, p.at(x=lax.rem(x + off, X))))
+        third.append(mine)
+    fourth = []
+    for step in range(Z):
+        line = lax.rem(z + Z - step, Z)
+        for copy in third[step]:
+            copy.wait_recv()
+        for off in range(1, C):
+            peer = p.at(c=lax.rem(c + off, C))
+            part = all_ref.at[line, :, :, c]
+            fourth.append(go(part, part, peer))
+            part = all_id_ref.at[line, :, :, c]
+            fourth.append(go(part, part, peer))
+    for copy in edges + fourth:
+        copy.wait_recv()
+    for copy in copies:
+        copy.wait_send()
+
+
+def gather_all(sizes, latent, ids, packed):
+    Z, Y, X, C = sizes
+    nodes, width = latent.shape
+    sends = (Z - 1) * 2 + 2 + Z * (3 * (X - 1) + 3 * (Y - 1) + 2 * (C - 1))
+    vmem = pl.BlockSpec(memory_space=pltpu.VMEM)
+    row = packed.shape[1:]
+    return pl.pallas_call(
+        functools.partial(gather_kernel, sizes),
+        out_shape=(
+            jax.ShapeDtypeStruct((Z, Y, X, C, nodes, width), latent.dtype),
+            jax.ShapeDtypeStruct((Z, Y, X, C, *ids.shape), ids.dtype),
+            jax.ShapeDtypeStruct(row, packed.dtype),
+            jax.ShapeDtypeStruct(row, packed.dtype),
+        ),
+        in_specs=[vmem] * 3,
+        out_specs=(vmem,) * 4,
+        scratch_shapes=[pltpu.SemaphoreType.DMA((2, sends))],
+        compiler_params=pltpu.CompilerParams(collective_id=0, has_side_effects=True),
+        name="gather_all",
+    )(latent, ids, packed)
+
+
+def reduce_kernel(sizes, *refs):
+    grads, refs = refs[:5], refs[5:]
+    out_ref, s1, r1, acc1, s2, r2, acc2, s3, r3, acc3, s4, r4, sq, zq, lq = refs[:15]
+    sem1, sem2, sem3, sem4, zsem, lsem = refs[15:]
+    p = Place(sizes)
+    Z, Y, X, C, z, y, x, c = p.Z, p.Y, p.X, p.C, p.z, p.y, p.x, p.c
+    many = len(grads)
+    w2 = out_ref.shape[-1] // 2
+    halves = (pl.ds(0, w2), pl.ds(w2, w2))
+    p.meet()
+    copies = []
+
+    def go(src, dst, sems, slot, peer):
+        copy = send(src, dst, sems, slot, peer)
+        copies.append(copy)
+        return copy
+
+    first = []
+    for m in range(many):
+        mine = []
+        for off in range(1, C):
+            there = lax.rem(c + off, C)
+            k = m * (C - 1) + off - 1
+            s1[k] = grads[m][:, :, :, there].astype(BF16)
+            mine.append((k, go(s1.at[k], r1.at[k], sem1, k, p.at(c=there))))
+        first.append(mine)
+    second = []
+    for m in range(many):
+        total = grads[m][:, :, :, c]
+        for k, copy in first[m]:
+            copy.wait_recv()
+            total = total + r1[k].astype(F32)
+        acc1[m] = total
+        mine = ([], [])
+        for off in range(1, X):
+            there = lax.rem(x + off, X)
+            k = m * (X - 1) + off - 1
+            s2[0][k] = acc1[m, :, :, there, :, halves[0]].astype(BF16)
+            mine[0].append((k, go(s2[0].at[k], r2[0].at[k], sem2[0], k, p.at(x=there))))
+        for off in range(1, Y):
+            there = lax.rem(y + off, Y)
+            k = m * (Y - 1) + off - 1
+            s2[1][k] = acc1[m, :, there, :, :, halves[1]].astype(BF16)
+            mine[1].append((k, go(s2[1].at[k], r2[1].at[k], sem2[1], k, p.at(y=there))))
+        second.append(mine)
+    third = []
+    for m in range(many):
+        mine = ([], [])
+        total = acc1[m, :, :, x, :, halves[0]]
+        for k, copy in second[m][0]:
+            copy.wait_recv()
+            total = total + r2[0][k].astype(F32)
+        acc2[0][m] = total
+        for off in range(1, Y):
+            there = lax.rem(y + off, Y)
+            k = m * (Y - 1) + off - 1
+            s3[0][k] = acc2[0][m, :, there].astype(BF16)
+            mine[0].append((k, go(s3[0].at[k], r3[0].at[k], sem3[0], k, p.at(y=there))))
+        total = acc1[m, :, y, :, :, halves[1]]
+        for k, copy in second[m][1]:
+            copy.wait_recv()
+            total = total + r2[1][k].astype(F32)
+        acc2[1][m] = total
+        for off in range(1, X):
+            there = lax.rem(x + off, X)
+            k = m * (X - 1) + off - 1
+            s3[1][k] = acc2[1][m, :, there].astype(BF16)
+            mine[1].append((k, go(s3[1].at[k], r3[1].at[k], sem3[1], k, p.at(x=there))))
+        third.append(mine)
+    fourth = []
+    for m in range(many):
+        for side, own in ((0, y), (1, x)):
+            total = acc2[side][m, :, own]
+            for k, copy in third[m][side]:
+                copy.wait_recv()
+                total = total + r3[side][k].astype(F32)
+            acc3[m, :, :, halves[side]] = total
+        mine = []
+        for off in range(1, Z):
+            there = lax.rem(z + off, Z)
+            k = m * (Z - 1) + off - 1
+            s4[k] = acc3[m, there].astype(BF16)
+            mine.append((k, go(s4.at[k], r4.at[k], sem4, k, (there, p.lon))))
+        fourth.append(mine)
+    square = jnp.zeros(out_ref.shape[1:], F32)
+    for m in range(many):
+        total = acc3[m, z]
+        for k, copy in fourth[m]:
+            copy.wait_recv()
+            total = total + r4[k].astype(F32)
+        out_ref[m] = total
+        square = square + total * total
+    sq[0] = jnp.broadcast_to(jnp.sum(square, keepdims=True), sq.shape[1:])
+    mine = []
+    for off in range(1, Z):
+        mine.append(go(sq.at[0], zq.at[off - 1], zsem, off - 1, (lax.rem(z + off, Z), p.lon)))
+    whole = sq[0]
+    for off, copy in enumerate(mine):
+        copy.wait_recv()
+        whole = whole + zq[off]
+    sq[1] = whole
+    mine = []
+    for off in range(1, p.L):
+        mine.append(go(sq.at[1], lq.at[off - 1], lsem, off - 1, (p.lat, lax.rem(p.lon + off, p.L))))
+    for off, copy in enumerate(mine):
+        copy.wait_recv()
+        whole = whole + lq[off]
+    norm = jnp.sqrt(whole[0:1, 0:1]) + 1e-06
+    for m in range(many):
+        out_ref[m] = out_ref[m] / norm
+    for copy in copies:
+        copy.wait_send()
+
+
+def reduce_all(sizes, grads):
+    Z, Y, X, C = sizes
+    L = Y * X * C
+    many = len(grads)
+    wide, width = grads[0].shape
+    R = wide // (Z * L)
+    w2 = width // 2
+    vmem = pl.BlockSpec(memory_space=pltpu.VMEM)
+
+    def buf(dtype, *dims):
+        return pltpu.VMEM(dims, dtype)
+
+    def two(count):
+        return [pltpu.SemaphoreType.DMA((2, n)) for n in count]
+
+    nx, ny, nz, nc = many * (X - 1), many * (Y - 1), many * (Z - 1), many * (C - 1)
+    second = [buf(BF16, nx, Z, Y, R, w2), buf(BF16, ny, Z, X, R, w2)]
+    third = [buf(BF16, ny, Z, R, w2), buf(BF16, nx, Z, R, w2)]
+    return pl.pallas_call(
+        functools.partial(reduce_kernel, sizes),
+        out_shape=jax.ShapeDtypeStruct((many, R, width), F32),
+        in_specs=[vmem] * many,
+        out_specs=vmem,
+        scratch_shapes=[
+            buf(BF16, nc, Z, Y, X, R, width), buf(BF16, nc, Z, Y, X, R, width),
+            buf(F32, many, Z, Y, X, R, width),
+            second, second, [buf(F32, many, Z, Y, R, w2), buf(F32, many, Z, X, R, w2)],
+            third, third, buf(F32, many, Z, R, width),
+            buf(BF16, nz, R, width), buf(BF16, nz, R, width),
+            buf(F32, 2, 8, 128), buf(F32, Z - 1, 8, 128), buf(F32, L - 1, 8, 128),
+            *two([nc]), two([nx, ny]), two([ny, nx]), *two([nz, Z - 1, L - 1]),
+        ],
+        compiler_params=pltpu.CompilerParams(
+            collective_id=1, has_side_effects=True, vmem_limit_bytes=60 * 1024 * 1024
+        ),
+        name="reduce_all",
+    )(*[grad.reshape(Z, Y, X, C, R, width) for grad in grads])
+
+
+def lon_parts(lat_count, lon_count):
+    chips = lon_count // 2
+    x = next(d for d in range(math.isqrt(chips), 0, -1) if chips % d == 0)
+    return lat_count, chips // x, x, 2
 
 
 def local(
@@ -83,12 +383,12 @@
     lat_count, lon_count = lax.axis_size("lat"), lax.axis_size("lon")
     latent = mesh_latent.reshape(nodes, width)
     ids = coarse_ids.reshape(nodes)
-    everyone = lax.all_gather(latent, AXES, axis=0, tiled=True)
-    all_ids = lax.all_gather(ids, AXES, axis=0, tiled=True)
+    sizes = lon_parts(lat_count, lon_count)
 
     own_target, packed = packed_edges(edge_source, edge_target, edge_owner, grid_rows, nodes)
-    from_right = shift(packed[0], "lon", -1)
-    from_left = shift(packed[1], "lon", 1)
+    everyone, all_ids, from_left, from_right = gather_all(sizes, latent, ids[None], packed[:, None])
+    everyone, all_ids = everyone.reshape(-1, width), all_ids.reshape(-1)
+    from_left, from_right = from_left[0], from_right[0]
     foreign = jnp.concatenate([from_left, from_right])
     offsets = jnp.repeat(jnp.array([1, 2], jnp.int32) * nodes, from_left.shape[0])
     every_target = jnp.concatenate([own_target, foreign % (grid_rows + 1) - 1])
@@ -144,12 +444,8 @@
     grad_source = mm_t(beside, d_edges.reshape(6 * nodes, width))
     d_sum = jnp.sum(d_edges.astype(F32), 0).astype(BF16)
     grad_target = mm_t(latent, d_sum)
-    stacked = jnp.stack([grad_source, grad_target, grad_node, grad_coarse, grad_decode]).reshape(
-        5, width * width
-    )
-    share = lax.psum_scatter(stacked, AXES, scatter_dimension=1, tiled=True)
-    norm = jnp.sqrt(lax.psum(jnp.sum(share * share), AXES))
-    clipped = share / (norm + 1e-06)
+    clipped = reduce_all(sizes, (grad_source, grad_target, grad_node, grad_coarse, grad_decode))
+    clipped = clipped.reshape(clipped.shape[0], -1)
     return (mesh_out.reshape(height, breadth, width), grid_out, clipped)
 
 

time: 317 us -> 101 us (0.32)
  waiting for transfers between devices: 149 us -> 0.01 us
  blocking collectives: 77.4 us -> 0 us
  Pallas kernels: 0 us -> 58.7 us
  local copies, waits for them, and re-layouts: 37.1 us -> 5.61 us
  between operations: 15.1 us -> 1.01 us
  matrix products: 19 us -> 22.7 us
    reduce_scatter x1 -> x0, waiting for transfers between devices: 143 us -> none  [local(): share = lax.psum_scatter(stacked, AXES, scatter_dimension=1, tiled=True)]
    pallas_call x0 -> x2, Pallas kernels: none -> 58.7 us  [the longest x1 34.9 us: reduce_all(): pl.pallas_call(functools.partial(reduce_kernel, sizes), out_shape=jax.Sha...]
    unnamed x1 -> x0, blocking collectives: 40.4 us -> none
    psum x1 -> x0, blocking collectives: 37 us -> none  [local(): norm = jnp.sqrt(lax.psum(jnp.sum(share * share), AXES))]
    another operation x1 -> x2, local copies, waits for them, and re-layouts: 20 us -> 1.18 us  [the longest x1 0.59 us: local(): ids[None]]
    unnamed x31 -> x40, local copies, waits for them, and re-layouts: 13.6 us -> 2.57 us
    dot_general x9, matrix products: 4.11 us -> 8.85 us  [mm_t(): lax.dot_general(left, right, (((0,), (0,)), ((), ())), preferred_element_...]
    all_gather x1 -> x0, waiting for transfers between devices: 3.7 us -> none  [local(): everyone = lax.all_gather(latent, AXES, axis=0, tiled=True)]
  transfers between devices with their start and end apart: 8 -> 4, of which waited for: 3 -> 0; matrix products, arithmetic and copies ran while one was open for 6% -> 18% of each run, Pallas kernels for 0% -> 35%
where the time goes in v2:
time: 101 us; the launch traced here: 100 us
  Pallas kernels  58.7 us (58%)
  matrix products  22.7 us (22%)
  other arithmetic  7.78 us (8%)
  local copies, waits for them, and re-layouts  5.61 us (6%)
  starting transfers between devices  4.25 us (4%)
  between operations  1.01 us (1%)
    pallas_call x1, Pallas kernels, reduce_all(): pl.pallas_call(functools.partial(reduce_kernel, sizes), out_shape=jax.Sha...  34.9 us
    pallas_call x1, Pallas kernels, gather_all(): pl.pallas_call(functools.partial(gather_kernel, sizes), out_shape=(jax.Sh...  23.8 us
    dot_general x10, matrix products, mm(): return jnp.dot(left, right, preferred_element_type=F32)  12.2 us
    dot_general x9, matrix products, mm_t(): lax.dot_general(left, right, (((0,), (0,)), ((), ())), preferred_element_...  8.85 us
    ppermute x4, starting transfers between devices, shift(): lax.ppermute(value, axis, [(i, (i + step) % count) for i in range(count)])  4.25 us
    unnamed x40, local copies, waits for them, and re-layouts  2.57 us
    pallas_call x3, other arithmetic, gather_all(): pl.pallas_call(functools.partial(gather_kernel, sizes), out_shape=(jax.Sh...  2.06 us
  transfers between devices with their start and end apart: 4, of which 0 were waited for; matrix products, arithmetic and copies ran while one was open for 18% of the time, Pallas kernels for 35%

profile of v2, /device:TPU:0, one launch (start us, length us, event | category | flops | bytes accessed | tf_op | source)
XLA Modules:
  0.0 100.1 jit_solution(18237246245061480800)
XLA Ops:
  0.6 0.0 copy-start
  0.7 0.8 compare_bitcast_fusion
  1.4 0.7 compare_convert_fusion.1
  2.1 0.1 select_reduce_fusion.1
  2.2 0.7 broadcast_in_dim.72
  3.0 0.5 broadcast.269
  3.5 1.3 %reduce.11 = s32[8,8]{1,0:T(8,128)S(1)} reduce(s32[8,8,1]{1,2,0:T(1,128)} %param.21, s32[]{:T(128)} %broadcast.269), dimensions={2}, to_apply=%param.21.reduce_sub_computation.5 | reduce | bytes 516 | tf_op args[8]
  4.8 0.6 broadcast_in_dim_reshape.4.id_ref
  5.4 0.8 bitcast_select_fusion
  6.2 0.1 select_reduce_fusion
  6.3 0.6 broadcast_in_dim_reshape.10.edge_ref
  6.9 23.8 %gather_all.1 = (bf16[4,2,2,2,64,512]{5,4,3,2,1,0:T(8,128)(2,1)}, s32[4,2,2,2,1,64]{5,4,3,2,1,0:T(1,128)}, s32[1,384]{1,0:T(1,128)}, s32[1,384]{1,0:T(1,128)}) custom-call(bf16[64,512]{1,0:T(8,128)(2,1)} %bitcast.78, s32[1,64]{1,0:T(1,128)} %broadcast_in_dim_reshape.4.id_ref, s32[2,1,384]{2,1,0:T(1,128)} %broadcast_in_dim_reshape.10.edge_ref), custom_call_target="tpu_custom_call" | custom-call | tf_op jit(solution)/shard_map/gather_all/pallas_call | solution.py:190
  30.7 0.7 reduce.4
  31.4 0.7 reduce.5
  32.1 0.7 pad_add_fusion.1
  32.8 3.9 %fusion = f32[1024,192]{0,1:T(8,128)S(1)} fusion(s32[3840]{0:T(1024)S(1)} %pad_add_fusion, s32[3840]{0:T(1024)S(1)} %pad_add_fusion.1), kind=kOutput, calls=%fused_computation.1 | convolution fusion | flops 1514618880 | bytes 817152 | tf_op jit(solution)/shard_map/dot_general | solution.py:22
  36.7 0.4 fusion.20
  37.1 0.0 copy-start.18
  37.1 0.0 copy-start.16
  37.1 0.0 copy-start.6
  37.2 0.0 copy-start.8
  37.2 1.1 %fusion.73 = (bf16[192,512]{1,0:T(8,128)(2,1)S(1)}, f32[192,512]{1,0:T(8,128)}) fusion(f32[192,512]{1,0:T(8,128)S(1)} %fusion.20, bf16[1024,512]{1,0:T(8,128)(2,1)S(1)} %copy-done, f32[1024,192]{0,1:T(8,128)S(1)} %fusion), kind=kOutput, calls=%fused_computation.147 | convolution fusion | flops 202506240 | bytes 2818048 | tf_op jit(solution)/shard_map/dot_general | solution.py:26
  38.3 0.7 fusion.72
  39.0 1.6 %collective-permute-start.2 = (bf16[64,512]{1,0:T(8,128)(2,1)}, bf16[64,512]{1,0:T(8,128)(2,1)}, u32[]{:S(2)}, u32[]{:S(2)}) collective-permute-start(bf16[64,512]{1,0:T(8,128)(2,1)} %get-tuple-element.13), channel_id=1, source_target_pairs={{0,7},{1,0},{2,1},{3,2},{4,3},{5,4},{6,5},{7,6},{8,15},{9,8},{10,9... | collective-permute-start | bytes 196616 | tf_op jit(solution)/shard_map/ppermute | solution.py:45
  40.5 0.0 collective-permute-start.3
  40.5 0.1 eq.133
  40.6 0.1 fusion.36
  40.7 0.1 eq.122
  40.8 0.2 fusion.59
  41.1 0.7 reduce.12
  41.8 0.1 eq.135
  41.8 0.2 convert_reduce_fusion
  42.1 2.2 %fusion.6 = bf16[64,512]{1,0:T(8,128)(2,1)S(1)} fusion(bf16[2048,512]{1,0:T(8,128)(2,1)} %bitcast.73, s32[2048]{0:T(1024)S(1)} %eq.135, s32[64]{0:T(128)S(1)} %eq.133, f32[64]{0:T(128)S(1)} %rsqrt.7), kind=kOutput, calls=%fused_computation.16 | convolution fusion | flops 134414336 | bytes 2171392 | tf_op jit(solution)/shard_map/dot_general | solution.py:22
  44.3 0.0 copy-start.9
  44.4 0.0 copy-start.10
  44.4 1.0 %fusion.5 = bf16[384,512]{1,0:T(8,128)(2,1)S(1)} fusion(bf16[2048,512]{1,0:T(8,128)(2,1)S(1)} %bitcast.74, s32[384]{0:T(512)S(1)} %eq.122), kind=kOutput, calls=%fused_computation.11 | convolution fusion | flops 806289408 | bytes 2491904 | tf_op jit(solution)/shard_map/dot_general | solution.py:22
  45.4 0.0 copy-done.9
  45.4 0.0 copy-start.11
  45.4 0.2 fusion.75
  45.7 0.4 fusion.74
  46.0 0.2 multiply_reduce_fusion
  46.3 0.2 copy-done.11
  46.5 0.9 add_convert_fusion.1
  47.4 0.2 copy.18
  47.6 0.0 copy-start.12
  47.6 1.4 %fusion.17 = (f32[64,512]{1,0:T(8,128)S(1)}, bf16[64,512]{1,0:T(8,128)(2,1)S(1)}) fusion(f32[192,512]{1,0:T(8,128)} %get-tuple-element.24, bf16[64,512]{1,0:T(8,128)(2,1)} %collective-permute-done.3, bf16[64,512]{1,0:T(8,128)(2,1)} %collective-permute-done.2, bf16[64,512]{1,0:T(8,128)(2,1)} %get-tuple-element.21, bf16[512,512]{1,0:T(8,128)(2,1)} %param.19), kind=kOutput, calls=%fused_computation.38 | convolution fusion | flops 34013184 | bytes 1048576 | tf_op jit(solution)/shard_map/dot_general | solution.py:22
  49.1 2.7 %collective-permute-start.1 = (bf16[64,512]{1,0:T(8,128)(2,1)S(1)}, bf16[64,512]{1,0:T(8,128)(2,1)S(1)}, u32[]{:S(2)}, u32[]{:S(2)}) collective-permute-start(bf16[64,512]{1,0:T(8,128)(2,1)S(1)} %get-tuple-element.16), channel_id=1, source_target_pairs={{0,7},{1,0},{2,1},{3,2},{4,3},{5,4},{6,5},{7,6},{8,15},{9,8},{10,9... | collective-permute-start | bytes 196616 | tf_op jit(solution)/shard_map/ppermute | solution.py:45
  51.8 0.0 collective-permute-start
  51.8 1.4 %fusion.7 = bf16[64,512]{1,0:T(8,128)(2,1)S(1)} fusion(bf16[512,512]{1,0:T(8,128)(2,1)} %param.19, f32[64,512]{1,0:T(8,128)} %get-tuple-element.22, f32[64,512]{1,0:T(8,128)S(1)} %get-tuple-element.15), kind=kOutput, calls=%fused_computation.17 | convolution fusion | flops 33882112 | bytes 851968 | tf_op jit(solution)/shard_map/dot_general | solution.py:30
  53.2 0.3 fusion.76
  53.5 0.3 fusion.13
  53.8 0.0 copy-start.13
  53.8 0.3 fusion.8
  54.1 1.3 %fusion.77 = f32[512,512]{1,0:T(8,128)} fusion(bf16[64,512]{1,0:T(8,128)(2,1)S(1)} %copy-done.15, bf16[64,512]{1,0:T(8,128)(2,1)S(1)} %fusion.7), kind=kOutput, calls=%fused_computation.151 | convolution fusion | flops 33554432 | bytes 1179648 | tf_op jit(solution)/shard_map/dot_general | solution.py:26
  55.4 0.3 fusion.24
  55.8 0.3 fusion.19
  56.1 1.3 %convolution_add_fusion.1 = f32[512,512]{1,0:T(8,128)} fusion(f32[512,512]{1,0:T(8,128)S(1)} %fusion.24, bf16[64,512]{1,0:T(8,128)(2,1)S(1)} %copy-done.5, f32[64,512]{1,0:T(8,128)S(1)} %copy-done.3, bf16[64,512]{1,0:T(8,128)(2,1)S(1)} %fusion.7), kind=kOutput, calls=%fused_computation.10 | convolution fusion | flops 34242560 | bytes 2359296 | tf_op jit(solution)/shard_map/dot_general | solution.py:26
  57.4 1.3 %convolution_add_fusion = f32[512,512]{1,0:T(8,128)} fusion(f32[512,512]{1,0:T(8,128)S(1)} %fusion.19, bf16[64,512]{1,0:T(8,128)(2,1)S(1)} %copy-done.13, f32[64,512]{1,0:T(8,128)S(1)} %get-tuple-element.15), kind=kOutput, calls=%fused_computation.9 | convolution fusion | flops 33849344 | bytes 2293760 | tf_op jit(solution)/shard_map/dot_general | solution.py:26
  58.7 1.4 %fusion.11.refs_0_ = f32[4,2,2,2,16,512]{5,4,3,2,1,0:T(8,128)} fusion(bf16[4,2,2,2,16,384]{5,4,3,2,1,0:T(8,128)(2,1)S(1)} %bitcast.75, bf16[384,512]{1,0:T(8,128)(2,1)S(1)} %fusion.8), kind=kOutput, calls=%fused_computation.30 | convolution fusion | flops 201326592 | bytes 1835008 | tf_op jit(solution)/shard_map/dot_general | solution.py:26
  60.1 1.4 %fusion.57 = f32[512,512]{0,1:T(8,128)} fusion(bf16[64,512]{1,0:T(8,128)(2,1)S(1)} %fusion.13, bf16[8,8,512]{2,1,0:T(8,128)(2,1)S(1)} %copy-done.7), kind=kOutput, calls=%fused_computation.131 | convolution fusion | flops 33554432 | bytes 1179648 | tf_op jit(solution)/shard_map/dot_general | solution.py:26
  61.5 34.9 %reduce_all.1 = f32[5,16,512]{2,1,0:T(8,128)} custom-call(f32[4,2,2,2,16,512]{5,4,3,2,1,0:T(8,128)} %fusion.11.refs_0_, f32[4,2,2,2,16,512]{5,4,3,2,1,0:T(8,128)} %bitcast.72, f32[4,2,2,2,16,512]{5,4,3,2,1,0:T(8,128)} %bitcast.69, f32[4,2,2,2,16,512]{5,4,3,2,1,0:T(8,128)} %bitcast.70, f32[4,2,2,2,16,512]{5,4,3,2,1,0:T(8,128)} %bitcast.71), custom_call_target="tpu_custom_call" | custom-call | tf_op jit(solution)/shard_map/reduce_all/pallas_call | solution.py:338
  96.4 1.7 %copy.20 = f32[1,5,16,512]{3,1,2,0:T(8,128)} copy(f32[1,5,16,512]{3,2,1,0:T(8,128)} %bitcast.77) | data formatting | bytes 327680
  98.2 0.5 fusion.18
  98.7 1.4 %add_convert_fusion = bf16[1024,512]{1,0:T(8,128)(2,1)} fusion(f32[1024,512]{1,0:T(8,128)S(1)} %fusion.18, bf16[64,512]{1,0:T(8,128)(2,1)S(1)} %collective-permute-done.1, bf16[64,512]{1,0:T(8,128)(2,1)S(1)} %collective-permute-done, bf16[64,512]{1,0:T(8,128)(2,1)S(1)} %get-tuple-element.16, f32[1024,192]{0,1:T(8,128)S(1)} %fusion), kind=kOutput, calls=%fused_computation.6 | convolution fusion | flops 203751424 | bytes 4128768 | tf_op jit(solution)/shard_map/dot_general | solution.py:22
  (38 shorter events, 0.1 us)
Async XLA Ops:
  0.6 36.1 %copy-start = (bf16[1024,512]{1,0:T(8,128)(2,1)S(1)}, bf16[1024,512]{1,0:T(8,128)(2,1)}, u32[]{:S(2)}) copy-start(bf16[1024,512]{1,0:T(8,128)(2,1)} %param.14) | copy-start | bytes 3145732
  37.1 3.4 %copy-start.18 = (s32[8,8,1]{1,2,0:T(1,128)S(1)}, s32[8,8,1]{1,2,0:T(1,128)}, u32[]{:S(2)}) copy-start(s32[8,8,1]{1,2,0:T(1,128)} %param.21) | copy-start | bytes 772
  37.1 3.5 %copy-start.16 = (s32[6,8,8]{2,1,0:T(8,128)S(1)}, s32[6,8,8]{2,1,0:T(8,128)}, u32[]{:S(2)}) copy-start(s32[6,8,8]{2,1,0:T(8,128)} %param.20) | copy-start | bytes 4612
  37.1 3.7 %copy-start.6 = (bf16[8,8,512]{2,1,0:T(8,128)(2,1)S(1)}, bf16[8,8,512]{2,1,0:T(8,128)(2,1)}, u32[]{:S(2)}) copy-start(bf16[8,8,512]{2,1,0:T(8,128)(2,1)} %param.13) | copy-start | bytes 196612
  37.2 3.7 %copy-start.8 = (bf16[512,512]{1,0:T(8,128)(2,1)S(1)}, bf16[512,512]{1,0:T(8,128)(2,1)}, u32[]{:S(2)}) copy-start(bf16[512,512]{1,0:T(8,128)(2,1)} %param.16) | copy-start | bytes 1572868
  37.2 3.9 %copy-start.17 = (s32[4,2,2,2,1,64]{5,4,3,2,1,0:T(1,128)S(1)}, s32[4,2,2,2,1,64]{5,4,3,2,1,0:T(1,128)}, u32[]{:S(2)}) copy-start(s32[4,2,2,2,1,64]{5,4,3,2,1,0:T(1,128)} %get-tuple-element.8) | copy-start | bytes 24580
  39.0 8.7 %collective-permute-start.2 = (bf16[64,512]{1,0:T(8,128)(2,1)}, bf16[64,512]{1,0:T(8,128)(2,1)}, u32[]{:S(2)}, u32[]{:S(2)}) collective-permute-start(bf16[64,512]{1,0:T(8,128)(2,1)} %get-tuple-element.13), channel_id=1, source_target_pairs={{0,7},{1,0},{2,1},{3,2},{4,3},{5,4},{6,5},{7,6},{8,15},{9,8},{10,9... | collective-permute-start | bytes 196616 | tf_op jit(solution)/shard_map/ppermute | solution.py:45
  40.5 7.1 %collective-permute-start.3 = (bf16[64,512]{1,0:T(8,128)(2,1)}, bf16[64,512]{1,0:T(8,128)(2,1)}, u32[]{:S(2)}, u32[]{:S(2)}) collective-permute-start(bf16[64,512]{1,0:T(8,128)(2,1)} %get-tuple-element.14), channel_id=1, source_target_pairs={{0,1},{1,2},{2,3},{3,4},{4,5},{5,6},{6,7},{7,0},{8,9},{9,10},{10,1... | collective-permute-start | bytes 196616 | tf_op jit(solution)/shard_map/ppermute | solution.py:45
  41.8 2.5 %copy-start.1 = (bf16[4,2,2,2,64,512]{5,4,3,2,1,0:T(8,128)(2,1)S(1)}, bf16[4,2,2,2,64,512]{5,4,3,2,1,0:T(8,128)(2,1)}, u32[]{:S(2)}) copy-start(bf16[4,2,2,2,64,512]{5,4,3,2,1,0:T(8,128)(2,1)} %get-tuple-element.7) | copy-start | bytes 6291460
  44.3 1.1 %copy-start.4 = (bf16[64,512]{1,0:T(8,128)(2,1)}, bf16[64,512]{1,0:T(8,128)(2,1)S(1)}, u32[]{:S(2)}) copy-start(bf16[64,512]{1,0:T(8,128)(2,1)S(1)} %fusion.6) | copy-start | bytes 196612
  44.3 1.1 %copy-start.9 = (bf16[512,512]{1,0:T(8,128)(2,1)S(1)}, bf16[512,512]{1,0:T(8,128)(2,1)}, u32[]{:S(2)}) copy-start(bf16[512,512]{1,0:T(8,128)(2,1)} %param.18) | copy-start | bytes 1572868
  44.4 1.3 %copy-start.10 = (bf16[512,512]{1,0:T(8,128)(2,1)S(1)}, bf16[512,512]{1,0:T(8,128)(2,1)}, u32[]{:S(2)}) copy-start(bf16[512,512]{1,0:T(8,128)(2,1)} %param.15) | copy-start | bytes 1572868
  45.4 1.1 %copy-start.11 = (bf16[512,512]{1,0:T(8,128)(2,1)S(1)}, bf16[512,512]{1,0:T(8,128)(2,1)}, u32[]{:S(2)}) copy-start(bf16[512,512]{1,0:T(8,128)(2,1)} %param.17) | copy-start | bytes 1572868
  45.6 1.8 %copy-start.2 = (f32[64,512]{1,0:T(8,128)}, f32[64,512]{1,0:T(8,128)S(1)}, u32[]{:S(2)}) copy-start(f32[64,512]{1,0:T(8,128)S(1)} %fusion.75) | copy-start | bytes 393220
  46.5 0.9 copy-start.14
  47.6 5.5 %copy-start.12 = (bf16[512,512]{1,0:T(8,128)(2,1)S(1)}, bf16[512,512]{1,0:T(8,128)(2,1)}, u32[]{:S(2)}) copy-start(bf16[512,512]{1,0:T(8,128)(2,1)} %param.17) | copy-start | bytes 1572868
  49.1 49.1 %collective-permute-start.1 = (bf16[64,512]{1,0:T(8,128)(2,1)S(1)}, bf16[64,512]{1,0:T(8,128)(2,1)S(1)}, u32[]{:S(2)}, u32[]{:S(2)}) collective-permute-start(bf16[64,512]{1,0:T(8,128)(2,1)S(1)} %get-tuple-element.16), channel_id=1, source_target_pairs={{0,7},{1,0},{2,1},{3,2},{4,3},{5,4},{6,5},{7,6},{8,15},{9,8},{10,9... | collective-permute-start | bytes 196616 | tf_op jit(solution)/shard_map/ppermute | solution.py:45
  51.8 46.4 %collective-permute-start = (bf16[64,512]{1,0:T(8,128)(2,1)S(1)}, bf16[64,512]{1,0:T(8,128)(2,1)S(1)}, u32[]{:S(2)}, u32[]{:S(2)}) collective-permute-start(bf16[64,512]{1,0:T(8,128)(2,1)S(1)} %get-tuple-element.16), channel_id=1, source_target_pairs={{0,1},{1,2},{2,3},{3,4},{4,5},{5,6},{6,7},{7,0},{8,9},{9,10},{10,1... | collective-permute-start | bytes 196616 | tf_op jit(solution)/shard_map/ppermute | solution.py:45
  51.8 2.3 %copy-start.15 = (bf16[64,512]{1,0:T(8,128)(2,1)S(1)}, bf16[64,512]{1,0:T(8,128)(2,1)}, u32[]{:S(2)}) copy-start(bf16[64,512]{1,0:T(8,128)(2,1)} %copy-done.14) | copy-start | bytes 196612
  53.2 2.3 %copy-start.3 = (f32[64,512]{1,0:T(8,128)S(1)}, f32[64,512]{1,0:T(8,128)}, u32[]{:S(2)}) copy-start(f32[64,512]{1,0:T(8,128)} %copy-done.2) | copy-start | bytes 393220
  53.2 2.2 %copy-start.5 = (bf16[64,512]{1,0:T(8,128)(2,1)S(1)}, bf16[64,512]{1,0:T(8,128)(2,1)}, u32[]{:S(2)}) copy-start(bf16[64,512]{1,0:T(8,128)(2,1)} %copy-done.4) | copy-start | bytes 196612
  53.8 2.0 %copy-start.13 = (bf16[64,512]{1,0:T(8,128)(2,1)S(1)}, bf16[64,512]{1,0:T(8,128)(2,1)}, u32[]{:S(2)}) copy-start(bf16[64,512]{1,0:T(8,128)(2,1)} %get-tuple-element.21) | copy-start | bytes 196612
  57.4 2.7 %copy-start.7 = (bf16[8,8,512]{2,1,0:T(8,128)(2,1)S(1)}, bf16[8,8,512]{2,1,0:T(8,128)(2,1)}, u32[]{:S(2)}) copy-start(bf16[8,8,512]{2,1,0:T(8,128)(2,1)} %param.13) | copy-start | bytes 196612

commit v3 on v2

v3 whole, which is shorter than its diff:
```python
import functools
import math

import jax
import jax.numpy as jnp
from jax import lax
from jax.experimental import pallas as pl
from jax.experimental.pallas import tpu as pltpu
from jax.sharding import PartitionSpec as P

CAP = 3
F32 = jnp.float32
BF16 = jnp.bfloat16


def silu_slope(value):
    sig = jax.nn.sigmoid(value)
    return sig * (1.0 + value * (1.0 - sig))


def mm(left, right):
    return jnp.dot(left, right, preferred_element_type=F32)


def mm_t(left, right):
    return lax.dot_general(left, right, (((0,), (0,)), ((), ())), preferred_element_type=F32)


def mm_nt(left, right):
    return lax.dot_general(left, right, (((1,), (1,)), ((), ())), preferred_element_type=F32)


def split_float(value):
    high = value.astype(BF16)
    return high, (value - high.astype(F32)).astype(BF16)


MESH = pl.DeviceIdType.MESH


class Place:
    def __init__(self, sizes):
        self.Z, self.Y, self.X, self.C = sizes
        self.L = self.Y * self.X * self.C
        self.lat, self.lon = lax.axis_index("lat"), lax.axis_index("lon")
        self.z, self.c = self.lat, lax.rem(self.lon, self.C)
        self.x = lax.rem(self.lon // self.C, self.X)
        self.y = self.lon // (self.C * self.X)

    def at(self, y=None, x=None, c=None):
        y, x, c = (old if new is None else new for new, old in ((y, self.y), (x, self.x), (c, self.c)))
        return (self.lat, (y * self.X + x) * self.C + c)

    def meet(self):
        barrier = pltpu.get_barrier_semaphore()
        for step in range(1, self.Z):
            peer = (lax.rem(self.z + step, self.Z), self.lon)
            pl.semaphore_signal(barrier, inc=1, device_id=peer, device_id_type=MESH)
        for step in range(1, self.L):
            peer = (self.lat, lax.rem(self.lon + step, self.L))
            pl.semaphore_signal(barrier, inc=1, device_id=peer, device_id_type=MESH)
        pl.semaphore_wait(barrier, self.Z - 1 + self.L - 1)


def send(src, dst, sems, slot, peer):
    copy = pltpu.make_async_remote_copy(
        src_ref=src, dst_ref=dst, send_sem=sems.at[0, slot], recv_sem=sems.at[1, slot],
        device_id=peer, device_id_type=MESH,
    )
    copy.start()
    return copy


def iota(shape, dim):
    return lax.broadcasted_iota(jnp.int32, shape, dim)


def step_kernel(sizes, *refs):
    (lat_ref, cot_ref, ws_ref, wt_ref, wn_ref, wc_ref, wd_ref, where_ref, id_ref, idcol_ref, src_ref, tgt_ref,
     owner_ref) = refs[:13]
    mesh_ref, grid_ref, out_ref = refs[13:16]
    (all_ref, all_id, near, pack, erow, counts, cnt_high, cnt_low, back, backs, msgs, grad, s1, r1, acc1, s2, r2, acc2,
     s3, r3, acc3, s4, r4, sq, zq, lq) = refs[16:42]
    gsem, esem, sem1, sem2, sem3, sem4, zsem, lsem = refs[42:]
    p = Place(sizes)
    Z, Y, X, C, z, y, x, c = p.Z, p.Y, p.X, p.C, p.z, p.y, p.x, p.c
    nodes, width = lat_ref.shape
    grid_rows = cot_ref.shape[0]
    blocks, block_len = src_ref.shape
    lanes = counts.shape[1]
    to_left = (p.lat, lax.rem(p.lon + p.L - 1, p.L))
    to_right = (p.lat, lax.rem(p.lon + 1, p.L))
    many = out_ref.shape[0]
    R = out_ref.shape[1]
    w2 = width // 2
    halves = (pl.ds(0, w2), pl.ds(w2, w2))
    half = nodes // 2
    low, high = pl.ds(0, half), pl.ds(half, half)
    copies = []
    used = [0]

    def go(src, dst, sems, slot, peer):
        copy = send(src, dst, sems, slot, peer)
        copies.append(copy)
        return copy

    def pass_on(src, dst, peer):
        used[0] += 1
        return go(src, dst, gsem, used[0] - 1, peer)

    all_ref[z, y, x, c] = lat_ref[...]
    all_id[z, y, x, c] = id_ref[...]
    owner = owner_ref[...]
    is_left = (owner == lax.rem(p.lon + p.L - 1, p.L)).astype(jnp.int32)
    is_right = (owner == lax.rem(p.lon + 1, p.L)).astype(jnp.int32)
    sub, lane = iota((blocks, blocks), 0), iota((blocks, blocks), 1)

    def ranks(column):
        row = jnp.sum(jnp.where(sub == lane, jnp.broadcast_to(column, sub.shape), 0), 0, keepdims=True)
        return jnp.sum(jnp.where(lane < sub, jnp.broadcast_to(row, sub.shape), 0), 1, keepdims=True)

    place = jnp.where(is_left == 1, ranks(is_left), jnp.where(is_right == 1, CAP + ranks(is_right), -1))
    wide_place = jnp.broadcast_to(place, (blocks, block_len))
    for r in range(2 * CAP):
        mine = wide_place == r
        side, row = divmod(r, CAP)
        pack[side, 0, row:row + 1] = jnp.sum(jnp.where(mine, src_ref[...], 0), 0, keepdims=True)
        pack[side, 1, row:row + 1] = jnp.sum(jnp.where(mine, tgt_ref[...] + 1, 0), 0, keepdims=True) - 1
    p.meet()
    first = []
    for step in range(1, Z):
        peer = (lax.rem(z + step, Z), p.lon)
        first.append([
            pass_on(lat_ref, all_ref.at[z, y, x, c], peer),
            pass_on(id_ref, all_id.at[z, y, x, c], peer),
        ])
    edges = [go(pack.at[0], pack.at[3], esem, 0, to_left), go(pack.at[1], pack.at[2], esem, 1, to_right)]
    second, third, fourth = [], [], []

    def hop_two(step):
        line = lax.rem(z + Z - step, Z)
        if step:
            for copy in first[step - 1]:
                copy.wait_recv()
        mine = []
        block = all_ref.at[line, y, x, c]
        src_low = block.at[low] if step else lat_ref.at[low]
        src_high = block.at[high] if step else lat_ref.at[high]
        src_id = all_id.at[line, y, x, c] if step else id_ref
        for off in range(1, X):
            peer = p.at(x=lax.rem(x + off, X))
            mine.append(pass_on(src_low, block.at[low], peer))
            mine.append(pass_on(src_id, all_id.at[line, y, x, c], peer))
        for off in range(1, Y):
            mine.append(pass_on(src_high, block.at[high], p.at(y=lax.rem(y + off, Y))))
        second.append(mine)

    def hop_three(step):
        line = lax.rem(z + Z - step, Z)
        for copy in second[step]:
            copy.wait_recv()
        mine = []
        for off in range(1, Y):
            peer = p.at(y=lax.rem(y + off, Y))
            part = all_ref.at[line, y, :, c, low]
            mine.append(pass_on(part, part, peer))
            part = all_id.at[line, y, :, c]
            mine.append(pass_on(part, part, peer))
        for off in range(1, X):
            part = all_ref.at[line, :, x, c, high]
            mine.append(pass_on(part, part, p.at(x=lax.rem(x + off, X))))
        third.append(mine)

    def hop_four(step):
        line = lax.rem(z + Z - step, Z)
        for copy in third[step]:
            copy.wait_recv()
        for off in range(1, C):
            peer = p.at(c=lax.rem(c + off, C))
            part = all_ref.at[line, :, :, c]
            fourth.append(pass_on(part, part, peer))
            part = all_id.at[line, :, :, c]
            fourth.append(pass_on(part, part, peer))

    stays = jnp.broadcast_to((owner == p.lon).astype(jnp.int32), (blocks, block_len))
    erow[0, 0:blocks] = src_ref[...]
    erow[1, 0:blocks] = jnp.where(stays == 1, tgt_ref[...], -1)
    pair = 2 if blocks % 2 == 0 else 1

    def count(start, stop):
        for b in range(start, stop, pair):
            upto = min(b + pair, stop)
            tgt = jnp.concatenate([jnp.broadcast_to(erow[1, r:r + 1], (grid_rows, block_len)) for r in range(b, upto)], 1)
            src = jnp.concatenate([jnp.broadcast_to(erow[0, r:r + 1], (lanes, block_len)) for r in range(b, upto)], 1)
            hot_t = jnp.where(tgt == iota(tgt.shape, 0), 1.0, 0.0).astype(BF16)
            hot_s = jnp.where(src == iota(src.shape, 0), 1.0, 0.0).astype(BF16)
            more = mm_nt(hot_t, hot_s)
            counts[...] = more if b == 0 else counts[...] + more

    hop_two(0)
    third_of = blocks // 3 // pair * pair
    count(0, third_of)
    for step in range(1, Z):
        hop_two(step)
    count(third_of, 2 * third_of)
    for step in range(Z):
        hop_three(step)
    count(2 * third_of, blocks)
    for copy in edges:
        copy.wait_recv()
    for side in range(2):
        erow[0, blocks + side * CAP:blocks + (side + 1) * CAP] = pack[2 + side, 0] + (side + 1) * nodes
        erow[1, blocks + side * CAP:blocks + (side + 1) * CAP] = pack[2 + side, 1]
    count(blocks, blocks + 2 * CAP)
    over = jnp.floor(counts[...] * (1.0 / 256.0)) * 256.0
    cnt_high[...] = over.astype(BF16)
    cnt_low[...] = (counts[...] - over).astype(BF16)
    cot_sums = mm_t(cnt_high[...], cot_ref[...]) + mm_t(cnt_low[...], cot_ref[...])
    backs[0] = cot_sums[nodes:2 * nodes].astype(BF16)
    backs[1] = cot_sums[2 * nodes:3 * nodes].astype(BF16)
    returns = [go(backs.at[0], back.at[0], esem, 2, to_left), go(backs.at[1], back.at[1], esem, 3, to_right)]
    for step in range(Z):
        hop_four(step)
    latent = lat_ref[...]
    toward = mm(latent, wt_ref[...])
    for copy in fourth:
        copy.wait_recv()

    for r in range(3):
        for q in range(3):
            lon = lax.rem(p.lon + q - 1 + p.L, p.L)
            line = lax.rem(z + r - 1 + Z, Z)
            block = all_ref[line, lon // (C * X), lax.rem(lon // C, X), lax.rem(lon, C)]
            near[(r * 3 + q) * nodes:(r * 3 + q + 1) * nodes] = block
    hot = jnp.broadcast_to(where_ref[...], (where_ref.shape[0], near.shape[0]))
    hot = jnp.where(hot == iota(hot.shape, 1), 1.0, 0.0).astype(BF16)
    beside = mm(hot, near[...]).astype(BF16)
    slots = beside.shape[0] // nodes
    edges_pre = mm(beside, ws_ref[...]).reshape(slots, nodes, width) + toward[None]
    agg = jnp.sum(edges_pre * jax.nn.sigmoid(edges_pre), 0).astype(BF16)

    pooled = jnp.zeros((nodes, width), F32)
    count_of = jnp.zeros((nodes, 1), F32)
    for line in range(Z):
        ids = jnp.sum(all_id[line].reshape(Y * X, C, C * nodes), 1)
        row = jnp.concatenate([ids[q:q + 1] for q in range(Y * X)], 1)
        wide = jnp.broadcast_to(row, (nodes, row.shape[1]))
        same = jnp.where(wide == jnp.broadcast_to(idcol_ref[...], wide.shape), 1.0, 0.0)
        count_of = count_of + jnp.sum(same, 1, keepdims=True)
        pooled = pooled + mm(same.astype(BF16), all_ref[line].reshape(p.L * nodes, width))
    coarse_in = (pooled * lax.rsqrt(count_of)).astype(BF16)
    cpre = mm(coarse_in, wc_ref[...])
    coarse_out = (cpre * jax.nn.sigmoid(cpre)).astype(BF16)
    npre = mm(agg, wn_ref[...]) + coarse_out.astype(F32)
    mesh_out = (latent.astype(F32) + npre * jax.nn.sigmoid(npre)).astype(BF16)
    mesh_ref[...] = mesh_out

    pre = mm(mesh_out, wd_ref[...])
    msgs[0:nodes] = (pre * jax.nn.sigmoid(pre)).astype(BF16)
    if lanes > 3 * nodes:
        msgs[3 * nodes:] = jnp.zeros((lanes - 3 * nodes, width), BF16)
    mine = msgs.at[pl.ds(0, nodes)]
    spoken = [
        go(mine, msgs.at[pl.ds(nodes, nodes)], esem, 4, to_right),
        go(mine, msgs.at[pl.ds(2 * nodes, nodes)], esem, 5, to_left),
    ]

    one, two, three, four = {}, {}, {}, {}

    def hop_core(m, value):
        if R % 8 == 0:
            grad[m] = value.reshape(Z, Y, X, C, R, width)
        else:
            for q in range(Z * p.L):
                spot = (q // p.L, q // (C * X) % Y, q // C % X, q % C)
                grad[(m, *spot)] = value[q * R:(q + 1) * R]
        one[m] = []
        for off in range(1, C):
            there = lax.rem(c + off, C)
            k = m * (C - 1) + off - 1
            s1[k] = grad[m, :, :, :, there].astype(BF16)
            one[m].append((k, go(s1.at[k], r1.at[k], sem1, k, p.at(c=there))))

    def hop_first(m):
        total = grad[m, :, :, :, c]
        for k, copy in one[m]:
            copy.wait_recv()
            total = total + r1[k].astype(F32)
        acc1[m] = total
        two[m] = ([], [])
        for off in range(1, X):
            there = lax.rem(x + off, X)
            k = m * (X - 1) + off - 1
            s2[0][k] = acc1[m, :, :, there, :, halves[0]].astype(BF16)
            two[m][0].append((k, go(s2[0].at[k], r2[0].at[k], sem2[0], k, p.at(x=there))))
        for off in range(1, Y):
            there = lax.rem(y + off, Y)
            k = m * (Y - 1) + off - 1
            s2[1][k] = acc1[m, :, there, :, :, halves[1]].astype(BF16)
            two[m][1].append((k, go(s2[1].at[k], r2[1].at[k], sem2[1], k, p.at(y=there))))

    def hop_other(m):
        three[m] = ([], [])
        total = acc1[m, :, :, x, :, halves[0]]
        for k, copy in two[m][0]:
            copy.wait_recv()
            total = total + r2[0][k].astype(F32)
        acc2[0][m] = total
        for off in range(1, Y):
            there = lax.rem(y + off, Y)
            k = m * (Y - 1) + off - 1
            s3[0][k] = acc2[0][m, :, there].astype(BF16)
            three[m][0].append((k, go(s3[0].at[k], r3[0].at[k], sem3[0], k, p.at(y=there))))
        total = acc1[m, :, y, :, :, halves[1]]
        for k, copy in two[m][1]:
            copy.wait_recv()
            total = total + r2[1][k].astype(F32)
        acc2[1][m] = total
        for off in range(1, X):
            there = lax.rem(x + off, X)
            k = m * (X - 1) + off - 1
            s3[1][k] = acc2[1][m, :, there].astype(BF16)
            three[m][1].append((k, go(s3[1].at[k], r3[1].at[k], sem3[1], k, p.at(x=there))))

    def hop_line(m):
        for side, own in ((0, y), (1, x)):
            total = acc2[side][m, :, own]
            for k, copy in three[m][side]:
                copy.wait_recv()
                total = total + r3[side][k].astype(F32)
            acc3[m, :, :, halves[side]] = total
        four[m] = []
        for off in range(1, Z):
            there = lax.rem(z + off, Z)
            k = m * (Z - 1) + off - 1
            s4[k] = acc3[m, there].astype(BF16)
            four[m].append((k, go(s4.at[k], r4.at[k], sem4, k, (there, p.lon))))

    for copy in returns:
        copy.wait_recv()
    cot_sum = cot_sums[:nodes] + back[0].astype(F32) + back[1].astype(F32)
    d_high, d_low = split_float(cot_sum * silu_slope(pre))
    hop_core(4, mm_t(mesh_out, d_high) + mm_t(mesh_out, d_low))
    d_node = (mm_nt(d_high, wd_ref[...]) * silu_slope(npre)).astype(BF16)
    hop_core(2, mm_t(agg, d_node))
    hop_first(4)
    c_high, c_low = split_float(d_node.astype(F32) * silu_slope(cpre))
    hop_core(3, mm_t(coarse_in, c_high) + mm_t(coarse_in, c_low))
    hop_first(2)
    d_edges = (mm_nt(d_node, wn_ref[...])[None] * silu_slope(edges_pre)).astype(BF16)
    d_sum = jnp.sum(d_edges.astype(F32), 0).astype(BF16)
    hop_core(1, mm_t(latent, d_sum))
    hop_first(3)
    hop_core(0, mm_t(beside, d_edges.reshape(slots * nodes, width)))
    hop_first(1)
    hop_first(0)
    order = (4, 2, 3, 1, 0)
    hop_other(order[0])
    for copy in spoken:
        copy.wait_recv()
    grid_ref[...] = (mm(cnt_high[...], msgs[...]) + mm(cnt_low[...], msgs[...])).astype(BF16)
    for m in order[1:]:
        hop_other(m)
    for m in order:
        hop_line(m)
    square = jnp.zeros(out_ref.shape[1:], F32)
    for m in order:
        total = acc3[m, z]
        for k, copy in four[m]:
            copy.wait_recv()
            total = total + r4[k].astype(F32)
        out_ref[m] = total
        square = square + total * total
    sq[0] = jnp.broadcast_to(jnp.sum(square, keepdims=True), sq.shape[1:])
    mine = []
    for off in range(1, Z):
        mine.append(go(sq.at[0], zq.at[off - 1], zsem, off - 1, (lax.rem(z + off, Z), p.lon)))
    whole = sq[0]
    for off, copy in enumerate(mine):
        copy.wait_recv()
        whole = whole + zq[off]
    sq[1] = whole
    mine = []
    for off in range(1, p.L):
        mine.append(go(sq.at[1], lq.at[off - 1], lsem, off - 1, (p.lat, lax.rem(p.lon + off, p.L))))
    for off, copy in enumerate(mine):
        copy.wait_recv()
        whole = whole + lq[off]
    norm = jnp.sqrt(whole[0:1, 0:1]) + 1e-06
    for m in range(many):
        out_ref[m] = out_ref[m] / norm
    for copy in copies:
        copy.wait_send()


def run_step(sizes, latent, cot, weights, where_idx, ids, id_column, source, target, owner):
    Z, Y, X, C = sizes
    L = Y * X * C
    many = len(weights)
    nodes, width = latent.shape
    grid_rows = cot.shape[0]
    blocks, block_len = source.shape
    lanes = -(-3 * nodes // 128) * 128
    R = width // (Z * L)
    w2 = width // 2
    vmem = pl.BlockSpec(memory_space=pltpu.VMEM)

    def buf(dtype, *dims):
        return pltpu.VMEM(dims, dtype)

    def sems(*counts):
        return [pltpu.SemaphoreType.DMA((2, n)) for n in counts]

    nx, ny, nz, nc = many * (X - 1), many * (Y - 1), many * (Z - 1), many * (C - 1)
    second = [buf(BF16, nx, Z, Y, R, w2), buf(BF16, ny, Z, X, R, w2)]
    third = [buf(BF16, ny, Z, R, w2), buf(BF16, nx, Z, R, w2)]
    gathers = (Z - 1) * 2 + Z * (3 * (X - 1) + 3 * (Y - 1) + 2 * (C - 1))
    return pl.pallas_call(
        functools.partial(step_kernel, sizes),
        out_shape=(
            jax.ShapeDtypeStruct((nodes, width), BF16),
            jax.ShapeDtypeStruct((grid_rows, width), BF16),
            jax.ShapeDtypeStruct((many, R, width), F32),
        ),
        in_specs=[vmem] * (8 + many),
        out_specs=(vmem,) * 3,
        scratch_shapes=[
            buf(BF16, Z, Y, X, C, nodes, width), buf(jnp.int32, Z, Y, X, C, *ids.shape),
            buf(BF16, 9 * nodes, width), buf(jnp.int32, 4, 2, CAP, block_len),
            buf(jnp.int32, 2, blocks + 2 * CAP, block_len),
            buf(F32, grid_rows, lanes), buf(BF16, grid_rows, lanes), buf(BF16, grid_rows, lanes),
            buf(BF16, 2, nodes, width), buf(BF16, 2, nodes, width), buf(BF16, lanes, width),
            buf(F32, many, Z, Y, X, C, R, width),
            buf(BF16, nc, Z, Y, X, R, width), buf(BF16, nc, Z, Y, X, R, width),
            buf(F32, many, Z, Y, X, R, width),
            second, second, [buf(F32, many, Z, Y, R, w2), buf(F32, many, Z, X, R, w2)],
            third, third, buf(F32, many, Z, R, width),
            buf(BF16, nz, R, width), buf(BF16, nz, R, width),
            buf(F32, 2, 8, 128), buf(F32, Z - 1, 8, 128), buf(F32, L - 1, 8, 128),
            *sems(gathers, 6, nc), sems(nx, ny), sems(ny, nx), *sems(nz, Z - 1, L - 1),
        ],
        compiler_params=pltpu.CompilerParams(
            collective_id=0, has_side_effects=True, vmem_limit_bytes=60 * 1024 * 1024
        ),
        name="whole_step",
    )(latent, cot, *weights, where_idx, ids, id_column, source, target, owner)


def lon_parts(lat_count, lon_count):
    chips = lon_count // 2
    x = next(d for d in range(math.isqrt(chips), 0, -1) if chips % d == 0)
    return lat_count, chips // x, x, 2


def local(
    mesh_latent,
    grid_cotangent,
    w_source,
    w_target,
    w_node,
    w_coarse,
    w_decode,
    neighbour_codes,
    coarse_ids,
    edge_source,
    edge_target,
    edge_owner,
):
    height, breadth, width = mesh_latent.shape
    nodes = height * breadth
    lat_pos, lon_pos = lax.axis_index("lat"), lax.axis_index("lon")
    lat_count, lon_count = lax.axis_size("lat"), lax.axis_size("lon")
    sizes = lon_parts(lat_count, lon_count)
    rows = jnp.arange(height, dtype=jnp.int32)[None, :, None] + neighbour_codes // 3 - 1
    cols = jnp.arange(breadth, dtype=jnp.int32)[None, None, :] + neighbour_codes % 3 - 1
    below, above = (rows < 0).astype(jnp.int32), (rows >= height).astype(jnp.int32)
    before, after = (cols < 0).astype(jnp.int32), (cols >= breadth).astype(jnp.int32)
    block = (1 + above - below) * 3 + 1 + after - before
    inner = (rows + height * (below - above)) * breadth + cols + breadth * (before - after)
    outside = (below == 1) & (lat_pos == 0) | (above == 1) & (lat_pos == lat_count - 1)
    where_idx = jnp.where(outside, -1, block * nodes + inner).reshape(-1, 1)
    cores = jnp.arange(sizes[3], dtype=jnp.int32)[:, None]
    ids = coarse_ids.reshape(1, nodes) + 1
    id_row = jnp.where(cores == lon_pos % sizes[3], ids, 0).reshape(1, -1)
    blocks = edge_owner.shape[0]
    mesh_out, grid_out, clipped = run_step(
        sizes,
        mesh_latent.reshape(nodes, width),
        grid_cotangent,
        (w_source, w_target, w_node, w_coarse, w_decode),
        where_idx,
        id_row,
        coarse_ids.reshape(nodes, 1) + 1,
        edge_source.reshape(blocks, -1),
        edge_target.reshape(blocks, -1),
        edge_owner,
    )
    return (mesh_out.reshape(height, breadth, width), grid_out, clipped.reshape(clipped.shape[0], -1))


def solution(mesh):
    in_specs = (
        P("lat", "lon", None),
        P(("lat", "lon"), None),
        P(),
        P(),
        P(),
        P(),
        P(),
        P(None, "lat", "lon"),
        P("lat", "lon", None),
        P(("lat", "lon")),
        P(("lat", "lon")),
        P(("lat", "lon"), None),
    )
    out_specs = (P("lat", "lon", None), P(("lat", "lon"), None), P(None, ("lat", "lon")))
    return jax.shard_map(local, mesh=mesh, in_specs=in_specs, out_specs=out_specs, check_vma=False)
```

time: 101 us -> 67.5 us (0.67)
  matrix products: 22.7 us -> 0 us
  other arithmetic: 7.78 us -> 0.16 us
  starting transfers between devices: 4.25 us -> 0 us
  local copies, waits for them, and re-layouts: 5.61 us -> 8.21 us
    dot_general x21 -> x0, matrix products: 22.7 us -> none  [the longest x10 12.2 us: mm(): return jnp.dot(left, right, preferred_element_type=F32)]
    ppermute x4 -> x0, starting transfers between devices: 4.25 us -> none  [shift(): lax.ppermute(value, axis, [(i, (i + step) % count) for i in range(count)])]
    unnamed x40 -> x12, local copies, waits for them, and re-layouts: 2.57 us -> 5.99 us
    pallas_call x3 -> x0, other arithmetic: 2.06 us -> none  [gather_all(): pl.pallas_call(functools.partial(gather_kernel, sizes), out_shape=(jax.Sh...]
    unnamed x1 -> x0, other arithmetic: 1.35 us -> none
    another operation x2 -> x0, local copies, waits for them, and re-layouts: 1.18 us -> none  [the longest x1 0.59 us: local(): ids[None]]
    pallas_call x2 -> x1, Pallas kernels: 58.7 us -> 58.2 us  [run_step(): pl.pallas_call(functools.partial(step_kernel, sizes), out_shape=(jax.Shap...]
  transfers between devices with their start and end apart: 4 -> 0, of which waited for: 0 -> 0; matrix products, arithmetic and copies ran while one was open for 18% -> 0% of each run, Pallas kernels for 35% -> 0%
where the time goes in v3:
time: 67.5 us; the launch traced here: 67.2 us
  Pallas kernels  58.2 us (86%)
  local copies, waits for them, and re-layouts  8.21 us (12%)
  between operations  0.69 us (1%)
    pallas_call x1, Pallas kernels, run_step(): pl.pallas_call(functools.partial(step_kernel, sizes), out_shape=(jax.Shap...  58.2 us
    unnamed x12, local copies, waits for them, and re-layouts  5.99 us

profile of v3, /device:TPU:0, one launch (start us, length us, event | category | flops | bytes accessed | tf_op | source)
XLA Modules:
  0.0 67.2 jit_solution(17172862314433557912)
XLA Ops:
  0.6 0.0 copy-start.2
  0.6 0.0 copy-start.1
  0.7 0.6 copy-done.2
  1.3 0.1 add.83
  1.4 0.1 broadcast_select_fusion
  1.5 0.7 select_n.41.refs_8_
  2.2 0.0 copy-done.1
  2.2 0.1 fusion.2
  2.2 0.8 %reshape.84.refs_7_ = s32[384,1]{1,0:T(8,128)} reshape(s32[6,8,8]{2,1,0:T(8,128)S(1)} %fusion.2) | data formatting | bytes 3072 | tf_op jit(solution)/shard_map/reshape | solution.py:481
  3.0 0.0 copy-start.3
  3.0 0.7 %add.85.refs_9_ = s32[64,1]{1,0:T(8,128)} reshape(s32[8,8]{1,0:T(8,128)S(1)} %bitcast.11) | data formatting | bytes 512 | tf_op jit(solution)/shard_map/add | solution.py:493
  3.7 0.0 copy-done.3
  3.7 0.7 %copy.19.refs_12_ = s32[24,1]{1,0:T(8,128)} copy(s32[24,1]{0,1:T(1,128)S(1)} %copy-done.3) | data formatting | bytes 192 | tf_op args[11]
  4.4 58.2 %whole_step.1 = (bf16[64,512]{1,0:T(8,128)(2,1)}, bf16[1024,512]{1,0:T(8,128)(2,1)}, f32[5,16,512]{2,1,0:T(8,128)}) custom-call(bf16[64,512]{1,0:T(8,128)(2,1)} %bitcast.9, bf16[1024,512]{1,0:T(8,128)(2,1)} %refs_1_.1, bf16[512,512]{1,0:T(8,128)(2,1)} %refs_2_.1, bf16[512,512]{1,0:T(8,128)(2,1)} %refs_3_.1, bf16[512,512]{1,0:T(8,128)(2,1)} %refs_4_.1, ...), custom_call_target="tpu_custom_call" | custom-call | tf_op jit(solution)/shard_map/whole_step/pallas_call | solution.py:418
  62.6 0.0 copy-start
  62.6 1.8 %copy.20 = f32[1,5,16,512]{3,1,2,0:T(8,128)} copy(f32[1,5,16,512]{3,2,1,0:T(8,128)} %bitcast.8) | data formatting | bytes 327680
  64.3 0.0 copy-done
  64.3 0.6 copy.23
  65.0 2.3 %copy.24 = bf16[1024,512]{1,0:T(8,128)(2,1)} copy(bf16[1024,512]{1,0:T(8,128)(2,1)} %get-tuple-element.15) | data formatting | bytes 2097152
  (2 shorter events, 0.0 us)
Async XLA Ops:
  0.6 0.7 %copy-start.2 = (s32[8,8,1]{1,2,0:T(1,128)S(1)}, s32[8,8,1]{1,2,0:T(1,128)}, u32[]{:S(2)}) copy-start(s32[8,8,1]{1,2,0:T(1,128)} %param.20) | copy-start | bytes 772
  0.6 1.5 %copy-start.1 = (s32[6,8,8]{2,1,0:T(8,128)S(1)}, s32[6,8,8]{2,1,0:T(8,128)}, u32[]{:S(2)}) copy-start(s32[6,8,8]{2,1,0:T(8,128)} %param.19) | copy-start | bytes 4612
  3.0 0.7 %copy-start.3 = (s32[24,1]{0,1:T(1,128)S(1)}, s32[24,1]{0,1:T(1,128)}, u32[]{:S(2)}) copy-start(s32[24,1]{0,1:T(1,128)} %param.23) | copy-start | bytes 292
  62.6 1.8 %copy-start = (bf16[64,512]{1,0:T(8,128)(2,1)S(1)}, bf16[64,512]{1,0:T(8,128)(2,1)}, u32[]{:S(2)}) copy-start(bf16[64,512]{1,0:T(8,128)(2,1)} %get-tuple-element.6) | copy-start | bytes 196612

commit v4 on v3

--- a/solution.py
+++ b/solution.py
@@ -59,7 +59,9 @@
         for step in range(1, self.L):
             peer = (self.lat, lax.rem(self.lon + step, self.L))
             pl.semaphore_signal(barrier, inc=1, device_id=peer, device_id_type=MESH)
-        pl.semaphore_wait(barrier, self.Z - 1 + self.L - 1)
+
+    def met(self):
+        pl.semaphore_wait(pltpu.get_barrier_semaphore(), self.Z - 1 + self.L - 1)
 
 
 def send(src, dst, sems, slot, peer):
@@ -76,12 +78,12 @@
 
 
 def step_kernel(sizes, *refs):
-    (lat_ref, cot_ref, ws_ref, wt_ref, wn_ref, wc_ref, wd_ref, where_ref, id_ref, idcol_ref, src_ref, tgt_ref,
-     owner_ref) = refs[:13]
-    mesh_ref, grid_ref, out_ref = refs[13:16]
+    (lat_ref, cot_ref, ws_ref, wt_ref, wn_ref, wc_ref, wd_ref, code_ref, coarse_ref, src_ref, tgt_ref,
+     owner_ref) = refs[:12]
+    mesh_ref, grid_ref, out_ref = refs[12:15]
     (all_ref, all_id, near, pack, erow, counts, cnt_high, cnt_low, back, backs, msgs, grad, s1, r1, acc1, s2, r2, acc2,
-     s3, r3, acc3, s4, r4, sq, zq, lq) = refs[16:42]
-    gsem, esem, sem1, sem2, sem3, sem4, zsem, lsem = refs[42:]
+     s3, r3, acc3, s4, r4, sq, zq, lq, id_ref, share) = refs[15:43]
+    gsem, esem, sem1, sem2, sem3, sem4, zsem, lsem = refs[43:]
     p = Place(sizes)
     Z, Y, X, C, z, y, x, c = p.Z, p.Y, p.X, p.C, p.z, p.y, p.x, p.c
     nodes, width = lat_ref.shape
@@ -91,7 +93,7 @@
     to_left = (p.lat, lax.rem(p.lon + p.L - 1, p.L))
     to_right = (p.lat, lax.rem(p.lon + 1, p.L))
     many = out_ref.shape[0]
-    R = out_ref.shape[1]
+    R = share.shape[1]
     w2 = width // 2
     halves = (pl.ds(0, w2), pl.ds(w2, w2))
     half = nodes // 2
@@ -108,12 +110,25 @@
         used[0] += 1
         return go(src, dst, gsem, used[0] - 1, peer)
 
+    p.meet()
     all_ref[z, y, x, c] = lat_ref[...]
+    slots, height, breadth = code_ref.shape
+
+    def column(square):
+        tall = jnp.concatenate([jnp.broadcast_to(square[i:i + 1], (breadth, breadth)) for i in range(height)], 0)
+        keep = iota(tall.shape, 0) % breadth == iota(tall.shape, 1)
+        return jnp.sum(jnp.where(keep, tall, 0), 1, keepdims=True)
+
+    id_column = column(coarse_ref[...]) + 1
+    spread = (nodes, id_ref.shape[1])
+    keep = iota(spread, 1) == iota(spread, 0) + c * nodes
+    id_ref[...] = jnp.sum(jnp.where(keep, jnp.broadcast_to(id_column, spread), 0), 0, keepdims=True)
     all_id[z, y, x, c] = id_ref[...]
-    owner = owner_ref[...]
+    sub, lane = iota((blocks, blocks), 0), iota((blocks, blocks), 1)
+    owner = jnp.broadcast_to(owner_ref[...], (blocks, blocks))
+    owner = jnp.sum(jnp.where(sub == lane, owner, 0), 1, keepdims=True)
     is_left = (owner == lax.rem(p.lon + p.L - 1, p.L)).astype(jnp.int32)
     is_right = (owner == lax.rem(p.lon + 1, p.L)).astype(jnp.int32)
-    sub, lane = iota((blocks, blocks), 0), iota((blocks, blocks), 1)
 
     def ranks(column):
         row = jnp.sum(jnp.where(sub == lane, jnp.broadcast_to(column, sub.shape), 0), 0, keepdims=True)
@@ -126,7 +141,7 @@
         side, row = divmod(r, CAP)
         pack[side, 0, row:row + 1] = jnp.sum(jnp.where(mine, src_ref[...], 0), 0, keepdims=True)
         pack[side, 1, row:row + 1] = jnp.sum(jnp.where(mine, tgt_ref[...] + 1, 0), 0, keepdims=True) - 1
-    p.meet()
+    p.met()
     first = []
     for step in range(1, Z):
         peer = (lax.rem(z + step, Z), p.lon)
@@ -175,12 +190,14 @@
         line = lax.rem(z + Z - step, Z)
         for copy in third[step]:
             copy.wait_recv()
+        mine = []
         for off in range(1, C):
             peer = p.at(c=lax.rem(c + off, C))
             part = all_ref.at[line, :, :, c]
-            fourth.append(pass_on(part, part, peer))
+            mine.append(pass_on(part, part, peer))
             part = all_id.at[line, :, :, c]
-            fourth.append(pass_on(part, part, peer))
+            mine.append(pass_on(part, part, peer))
+        fourth.append(mine)
 
     stays = jnp.broadcast_to((owner == p.lon).astype(jnp.int32), (blocks, block_len))
     erow[0, 0:blocks] = src_ref[...]
@@ -197,15 +214,18 @@
             more = mm_nt(hot_t, hot_s)
             counts[...] = more if b == 0 else counts[...] + more
 
+    quarter = blocks // 4 // pair * pair
     hop_two(0)
-    third_of = blocks // 3 // pair * pair
-    count(0, third_of)
+    count(0, quarter)
     for step in range(1, Z):
         hop_two(step)
-    count(third_of, 2 * third_of)
+    count(quarter, 2 * quarter)
     for step in range(Z):
         hop_three(step)
-    count(2 * third_of, blocks)
+    count(2 * quarter, 3 * quarter)
+    for step in range(Z):
+        hop_four(step)
+    count(3 * quarter, blocks)
     for copy in edges:
         copy.wait_recv()
     for side in range(2):
@@ -219,12 +239,24 @@
     backs[0] = cot_sums[nodes:2 * nodes].astype(BF16)
     backs[1] = cot_sums[2 * nodes:3 * nodes].astype(BF16)
     returns = [go(backs.at[0], back.at[0], esem, 2, to_left), go(backs.at[1], back.at[1], esem, 3, to_right)]
-    for step in range(Z):
-        hop_four(step)
     latent = lat_ref[...]
     toward = mm(latent, wt_ref[...])
-    for copy in fourth:
-        copy.wait_recv()
+
+    pooled = jnp.zeros((nodes, width), F32)
+    count_of = jnp.zeros((nodes, 1), F32)
+    for step in range(Z):
+        line = lax.rem(z + Z - step, Z)
+        for copy in fourth[step]:
+            copy.wait_recv()
+        ids = jnp.sum(all_id[line].reshape(Y * X, C, C * nodes), 1)
+        row = jnp.concatenate([ids[q:q + 1] for q in range(Y * X)], 1)
+        wide = jnp.broadcast_to(row, (nodes, row.shape[1]))
+        same = jnp.where(wide == jnp.broadcast_to(id_column, wide.shape), 1.0, 0.0)
+        count_of = count_of + jnp.sum(same, 1, keepdims=True)
+        pooled = pooled + mm(same.astype(BF16), all_ref[line].reshape(p.L * nodes, width))
+    coarse_in = (pooled * lax.rsqrt(count_of)).astype(BF16)
+    cpre = mm(coarse_in, wc_ref[...])
+    coarse_out = (cpre * jax.nn.sigmoid(cpre)).astype(BF16)
 
     for r in range(3):
         for q in range(3):
@@ -232,25 +264,26 @@
             line = lax.rem(z + r - 1 + Z, Z)
             block = all_ref[line, lon // (C * X), lax.rem(lon // C, X), lax.rem(lon, C)]
             near[(r * 3 + q) * nodes:(r * 3 + q + 1) * nodes] = block
-    hot = jnp.broadcast_to(where_ref[...], (where_ref.shape[0], near.shape[0]))
+    at_row, at_col = iota((height, breadth), 0), iota((height, breadth), 1)
+    wheres = []
+    for k in range(slots):
+        code = code_ref[k]
+        down = jnp.where(code >= 6, 1, jnp.where(code >= 3, 0, -1))
+        rows, cols = at_row + down, at_col + code - 3 * down - 4
+        below, above = jnp.where(rows < 0, 1, 0), jnp.where(rows >= height, 1, 0)
+        before, after = jnp.where(cols < 0, 1, 0), jnp.where(cols >= breadth, 1, 0)
+        block = (1 + above - below) * 3 + 1 + after - before
+        inner = (rows + height * (below - above)) * breadth + cols + breadth * (before - after)
+        first_line, last_line = jnp.where(z == 0, 1, 0), jnp.where(z == Z - 1, 1, 0)
+        outside = below * first_line + above * last_line
+        wheres.append(column(jnp.where(outside > 0, -1, block * nodes + inner)))
+    where = jnp.concatenate(wheres, 0)
+    hot = jnp.broadcast_to(where, (where.shape[0], near.shape[0]))
     hot = jnp.where(hot == iota(hot.shape, 1), 1.0, 0.0).astype(BF16)
     beside = mm(hot, near[...]).astype(BF16)
-    slots = beside.shape[0] // nodes
     edges_pre = mm(beside, ws_ref[...]).reshape(slots, nodes, width) + toward[None]
     agg = jnp.sum(edges_pre * jax.nn.sigmoid(edges_pre), 0).astype(BF16)
 
-    pooled = jnp.zeros((nodes, width), F32)
-    count_of = jnp.zeros((nodes, 1), F32)
-    for line in range(Z):
-        ids = jnp.sum(all_id[line].reshape(Y * X, C, C * nodes), 1)
-        row = jnp.concatenate([ids[q:q + 1] for q in range(Y * X)], 1)
-        wide = jnp.broadcast_to(row, (nodes, row.shape[1]))
-        same = jnp.where(wide == jnp.broadcast_to(idcol_ref[...], wide.shape), 1.0, 0.0)
-        count_of = count_of + jnp.sum(same, 1, keepdims=True)
-        pooled = pooled + mm(same.astype(BF16), all_ref[line].reshape(p.L * nodes, width))
-    coarse_in = (pooled * lax.rsqrt(count_of)).astype(BF16)
-    cpre = mm(coarse_in, wc_ref[...])
-    coarse_out = (cpre * jax.nn.sigmoid(cpre)).astype(BF16)
     npre = mm(agg, wn_ref[...]) + coarse_out.astype(F32)
     mesh_out = (latent.astype(F32) + npre * jax.nn.sigmoid(npre)).astype(BF16)
     mesh_ref[...] = mesh_out
@@ -363,13 +396,13 @@
         hop_other(m)
     for m in order:
         hop_line(m)
-    square = jnp.zeros(out_ref.shape[1:], F32)
+    square = jnp.zeros(share.shape[1:], F32)
     for m in order:
         total = acc3[m, z]
         for k, copy in four[m]:
             copy.wait_recv()
             total = total + r4[k].astype(F32)
-        out_ref[m] = total
+        share[m] = total
         square = square + total * total
     sq[0] = jnp.broadcast_to(jnp.sum(square, keepdims=True), sq.shape[1:])
     mine = []
@@ -388,12 +421,14 @@
         whole = whole + lq[off]
     norm = jnp.sqrt(whole[0:1, 0:1]) + 1e-06
     for m in range(many):
-        out_ref[m] = out_ref[m] / norm
+        total = share[m] / norm
+        for r in range(R):
+            out_ref[m:m + 1, r * width:(r + 1) * width] = total[r:r + 1]
     for copy in copies:
         copy.wait_send()
 
 
-def run_step(sizes, latent, cot, weights, where_idx, ids, id_column, source, target, owner):
+def run_step(sizes, latent, cot, weights, codes, ids, source, target, owner):
     Z, Y, X, C = sizes
     L = Y * X * C
     many = len(weights)
@@ -420,12 +455,12 @@
         out_shape=(
             jax.ShapeDtypeStruct((nodes, width), BF16),
             jax.ShapeDtypeStruct((grid_rows, width), BF16),
-            jax.ShapeDtypeStruct((many, R, width), F32),
+            jax.ShapeDtypeStruct((many, R * width), F32),
         ),
-        in_specs=[vmem] * (8 + many),
+        in_specs=[vmem] * (7 + many),
         out_specs=(vmem,) * 3,
         scratch_shapes=[
-            buf(BF16, Z, Y, X, C, nodes, width), buf(jnp.int32, Z, Y, X, C, *ids.shape),
+            buf(BF16, Z, Y, X, C, nodes, width), buf(jnp.int32, Z, Y, X, C, 1, C * nodes),
             buf(BF16, 9 * nodes, width), buf(jnp.int32, 4, 2, CAP, block_len),
             buf(jnp.int32, 2, blocks + 2 * CAP, block_len),
             buf(F32, grid_rows, lanes), buf(BF16, grid_rows, lanes), buf(BF16, grid_rows, lanes),
@@ -437,13 +472,14 @@
             third, third, buf(F32, many, Z, R, width),
             buf(BF16, nz, R, width), buf(BF16, nz, R, width),
             buf(F32, 2, 8, 128), buf(F32, Z - 1, 8, 128), buf(F32, L - 1, 8, 128),
+            buf(jnp.int32, 1, C * nodes), buf(F32, many, R, width),
             *sems(gathers, 6, nc), sems(nx, ny), sems(ny, nx), *sems(nz, Z - 1, L - 1),
         ],
         compiler_params=pltpu.CompilerParams(
             collective_id=0, has_side_effects=True, vmem_limit_bytes=60 * 1024 * 1024
         ),
         name="whole_step",
-    )(latent, cot, *weights, where_idx, ids, id_column, source, target, owner)
+    )(latent, cot, *weights, codes, ids, source, target, owner)
 
 
 def lon_parts(lat_count, lon_count):
@@ -468,34 +504,20 @@
 ):
     height, breadth, width = mesh_latent.shape
     nodes = height * breadth
-    lat_pos, lon_pos = lax.axis_index("lat"), lax.axis_index("lon")
-    lat_count, lon_count = lax.axis_size("lat"), lax.axis_size("lon")
-    sizes = lon_parts(lat_count, lon_count)
-    rows = jnp.arange(height, dtype=jnp.int32)[None, :, None] + neighbour_codes // 3 - 1
-    cols = jnp.arange(breadth, dtype=jnp.int32)[None, None, :] + neighbour_codes % 3 - 1
-    below, above = (rows < 0).astype(jnp.int32), (rows >= height).astype(jnp.int32)
-    before, after = (cols < 0).astype(jnp.int32), (cols >= breadth).astype(jnp.int32)
-    block = (1 + above - below) * 3 + 1 + after - before
-    inner = (rows + height * (below - above)) * breadth + cols + breadth * (before - after)
-    outside = (below == 1) & (lat_pos == 0) | (above == 1) & (lat_pos == lat_count - 1)
-    where_idx = jnp.where(outside, -1, block * nodes + inner).reshape(-1, 1)
-    cores = jnp.arange(sizes[3], dtype=jnp.int32)[:, None]
-    ids = coarse_ids.reshape(1, nodes) + 1
-    id_row = jnp.where(cores == lon_pos % sizes[3], ids, 0).reshape(1, -1)
+    sizes = lon_parts(lax.axis_size("lat"), lax.axis_size("lon"))
     blocks = edge_owner.shape[0]
     mesh_out, grid_out, clipped = run_step(
         sizes,
         mesh_latent.reshape(nodes, width),
         grid_cotangent,
         (w_source, w_target, w_node, w_coarse, w_decode),
-        where_idx,
-        id_row,
-        coarse_ids.reshape(nodes, 1) + 1,
+        neighbour_codes,
+        coarse_ids.reshape(height, breadth),
         edge_source.reshape(blocks, -1),
         edge_target.reshape(blocks, -1),
-        edge_owner,
+        edge_owner.reshape(1, blocks),
     )
-    return (mesh_out.reshape(height, breadth, width), grid_out, clipped.reshape(clipped.shape[0], -1))
+    return (mesh_out.reshape(height, breadth, width), grid_out, clipped)
 
 
 def solution(mesh):

time: 67.5 us -> 65.1 us (0.964)
  local copies, waits for them, and re-layouts: 8.21 us -> 4.48 us
  Pallas kernels: 58.2 us -> 59.8 us
    pallas_call x1, Pallas kernels: 58.2 us -> 59.8 us  [run_step(): pl.pallas_call(functools.partial(step_kernel, sizes), out_shape=(jax.Shap...]
    unnamed x12 -> x5, local copies, waits for them, and re-layouts: 5.99 us -> 4.48 us
    reshape x1 -> x0, local copies, waits for them, and re-layouts: 0.79 us -> none  [local(): where_idx = jnp.where(outside, -1, block * nodes + inner).reshape(-1, 1)]
    add x2 -> x0, local copies, waits for them, and re-layouts: 0.77 us -> none  [the longest x1 0.69 us: local(): coarse_ids.reshape(nodes, 1) + 1]
where the time goes in v4:
time: 65.1 us; the launch traced here: 64.9 us
  Pallas kernels  59.8 us (92%)
  local copies, waits for them, and re-layouts  4.48 us (7%)
    pallas_call x1, Pallas kernels, run_step(): pl.pallas_call(functools.partial(step_kernel, sizes), out_shape=(jax.Shap...  59.8 us
    unnamed x5, local copies, waits for them, and re-layouts  4.48 us

profile of v4, /device:TPU:0, one launch (start us, length us, event | category | flops | bytes accessed | tf_op | source)
XLA Modules:
  0.0 64.9 jit_solution(2631484156770942673)
XLA Ops:
  0.6 59.8 %whole_step.1 = (bf16[64,512]{1,0:T(8,128)(2,1)}, bf16[1024,512]{1,0:T(8,128)(2,1)}, f32[5,8192]{1,0:T(8,128)}) custom-call(bf16[64,512]{1,0:T(8,128)(2,1)} %bitcast.6, bf16[1024,512]{1,0:T(8,128)(2,1)} %refs_1_.1, bf16[512,512]{1,0:T(8,128)(2,1)} %refs_2_.1, bf16[512,512]{1,0:T(8,128)(2,1)} %refs_3_.1, bf16[512,512]{1,0:T(8,128)(2,1)} %refs_4_.1, ...), custom_call_target="tpu_custom_call" | custom-call | tf_op jit(solution)/shard_map/whole_step/pallas_call | solution.py:453
  60.4 1.5 %copy.18 = bf16[8,8,512]{2,1,0:T(8,128)(2,1)} copy(bf16[8,8,512]{2,1,0:T(8,128)(2,1)} %bitcast.7) | data formatting | bytes 131072
  61.9 0.0 copy-start
  61.9 2.3 %copy.19 = bf16[1024,512]{1,0:T(8,128)(2,1)} copy(bf16[1024,512]{1,0:T(8,128)(2,1)} %get-tuple-element.13) | data formatting | bytes 2097152
  64.2 0.0 copy-done
  64.2 0.7 %copy.20 = f32[5,8192]{1,0:T(8,128)} copy(f32[5,8192]{1,0:T(8,128)S(1)} %copy-done) | data formatting | bytes 327680
Async XLA Ops:
  61.9 2.3 %copy-start = (f32[5,8192]{1,0:T(8,128)S(1)}, f32[5,8192]{1,0:T(8,128)}, u32[]{:S(2)}) copy-start(f32[5,8192]{1,0:T(8,128)} %get-tuple-element.14) | copy-start | bytes 491524

commit v5 on v4

--- a/solution.py
+++ b/solution.py
@@ -476,10 +476,32 @@
             *sems(gathers, 6, nc), sems(nx, ny), sems(ny, nx), *sems(nz, Z - 1, L - 1),
         ],
         compiler_params=pltpu.CompilerParams(
-            collective_id=0, has_side_effects=True, vmem_limit_bytes=60 * 1024 * 1024
+            collective_id=0, has_side_effects=True, vmem_limit_bytes=48 * 1024 * 1024
         ),
         name="whole_step",
     )(latent, cot, *weights, codes, ids, source, target, owner)
+
+
+def write_kernel(*refs):
+    count = len(refs) // 2
+    sems = refs[-1]
+    moves = [pltpu.make_async_copy(refs[i], refs[count + i], sems.at[i]) for i in range(count)]
+    for move in moves:
+        move.start()
+    for move in moves:
+        move.wait()
+
+
+def write_results(*results):
+    return pl.pallas_call(
+        write_kernel,
+        out_shape=tuple(jax.ShapeDtypeStruct(r.shape, r.dtype) for r in results),
+        in_specs=[pl.BlockSpec(memory_space=pltpu.VMEM)] * len(results),
+        out_specs=(pl.BlockSpec(memory_space=pl.ANY),) * len(results),
+        scratch_shapes=[pltpu.SemaphoreType.DMA((len(results),))],
+        compiler_params=pltpu.CompilerParams(vmem_limit_bytes=8 * 1024 * 1024),
+        name="write_results",
+    )(*results)
 
 
 def lon_parts(lat_count, lon_count):
@@ -517,6 +539,7 @@
         edge_target.reshape(blocks, -1),
         edge_owner.reshape(1, blocks),
     )
+    mesh_out, grid_out, clipped = write_results(mesh_out, grid_out, clipped)
     return (mesh_out.reshape(height, breadth, width), grid_out, clipped)
 
 

time: 65.1 us -> 69.1 us (1.061)
  local copies, waits for them, and re-layouts: 4.48 us -> 10.1 us
  Pallas kernels: 59.8 us -> 57.7 us
    unnamed x5 -> x24, local copies, waits for them, and re-layouts: 4.48 us -> 10.1 us
    pallas_call x1, Pallas kernels: 59.8 us -> 56.6 us  [run_step(): pl.pallas_call(functools.partial(step_kernel, sizes), out_shape=(jax.Shap...]
    pallas_call x0 -> x1, Pallas kernels: none -> 1.1 us  [write_results(): pl.pallas_call(write_kernel, out_shape=tuple((jax.ShapeDtypeStruct(r.shap...]
where the time goes in v5:
time: 69.1 us; the launch traced here: 68.5 us
  Pallas kernels  57.7 us (84%)
  local copies, waits for them, and re-layouts  10.1 us (15%)
    pallas_call x1, Pallas kernels, run_step(): pl.pallas_call(functools.partial(step_kernel, sizes), out_shape=(jax.Shap...  56.6 us
    unnamed x24, local copies, waits for them, and re-layouts  10.1 us

profile of v5, /device:TPU:0, one launch (start us, length us, event | category | flops | bytes accessed | tf_op | source)
XLA Modules:
  0.0 68.5 jit_solution(7095962624284530330)
XLA Ops:
  0.6 0.0 copy-start.10
  0.6 0.0 copy-start.11
  0.7 0.7 copy-done.10
  1.3 0.0 copy-done.11
  1.3 0.0 copy-start
  1.3 1.2 %copy-done = bf16[1024,512]{1,0:T(8,128)(2,1)S(1)} copy-done((bf16[1024,512]{1,0:T(8,128)(2,1)S(1)}, bf16[1024,512]{1,0:T(8,128)(2,1)}, u32[]{:S(2)}) %copy-start) | copy-done | bytes 1048600
  2.6 0.0 copy-start.1
  2.6 1.0 %copy-done.1 = bf16[512,512]{1,0:T(8,128)(2,1)S(1)} copy-done((bf16[512,512]{1,0:T(8,128)(2,1)S(1)}, bf16[512,512]{1,0:T(8,128)(2,1)}, u32[]{:S(2)}) %copy-start.1) | copy-done | bytes 524312
  3.6 0.0 copy-start.2
  3.6 1.0 %copy-done.2 = bf16[512,512]{1,0:T(8,128)(2,1)S(1)} copy-done((bf16[512,512]{1,0:T(8,128)(2,1)S(1)}, bf16[512,512]{1,0:T(8,128)(2,1)}, u32[]{:S(2)}) %copy-start.2) | copy-done | bytes 524312
  4.6 0.0 copy-start.3
  4.6 1.0 %copy-done.3 = bf16[512,512]{1,0:T(8,128)(2,1)S(1)} copy-done((bf16[512,512]{1,0:T(8,128)(2,1)S(1)}, bf16[512,512]{1,0:T(8,128)(2,1)}, u32[]{:S(2)}) %copy-start.3) | copy-done | bytes 524312
  5.7 0.0 copy-start.4
  5.7 1.0 %copy-done.4 = bf16[512,512]{1,0:T(8,128)(2,1)S(1)} copy-done((bf16[512,512]{1,0:T(8,128)(2,1)S(1)}, bf16[512,512]{1,0:T(8,128)(2,1)}, u32[]{:S(2)}) %copy-start.4) | copy-done | bytes 524312
  6.7 0.0 copy-start.5
  6.7 1.0 %copy-done.5 = bf16[512,512]{1,0:T(8,128)(2,1)S(1)} copy-done((bf16[512,512]{1,0:T(8,128)(2,1)S(1)}, bf16[512,512]{1,0:T(8,128)(2,1)}, u32[]{:S(2)}) %copy-start.5) | copy-done | bytes 524312
  7.8 0.0 copy-start.6
  7.8 0.8 %copy-done.6 = bf16[8,8,512]{2,1,0:T(8,128)(2,1)S(1)} copy-done((bf16[8,8,512]{2,1,0:T(8,128)(2,1)S(1)}, bf16[8,8,512]{2,1,0:T(8,128)(2,1)}, u32[]{:S(2)}) %copy-start.6) | copy-done | bytes 65560
  8.6 0.0 copy-start.7
  8.6 0.7 %copy-done.7 = s32[6,8,8]{2,1,0:T(8,128)S(1)} copy-done((s32[6,8,8]{2,1,0:T(8,128)S(1)}, s32[6,8,8]{2,1,0:T(8,128)}, u32[]{:S(2)}) %copy-start.7) | copy-done | bytes 1560
  9.3 0.0 copy-start.8
  9.3 0.7 %copy-done.8 = s32[3072]{0:T(1024)S(1)} copy-done((s32[3072]{0:T(1024)S(1)}, s32[3072]{0:T(1024)}, u32[]{:S(2)}) %copy-start.8) | copy-done | bytes 12312
  10.0 0.0 copy-start.9
  10.0 0.7 %copy-done.9 = s32[3072]{0:T(1024)S(1)} copy-done((s32[3072]{0:T(1024)S(1)}, s32[3072]{0:T(1024)}, u32[]{:S(2)}) %copy-start.9) | copy-done | bytes 12312
  10.8 56.6 %whole_step.1 = (bf16[64,512]{1,0:T(8,128)(2,1)S(1)}, bf16[1024,512]{1,0:T(8,128)(2,1)S(1)}, f32[5,8192]{1,0:T(8,128)S(1)}) custom-call(bf16[64,512]{1,0:T(8,128)(2,1)S(1)} %bitcast.6, bf16[1024,512]{1,0:T(8,128)(2,1)S(1)} %copy-done, bf16[512,512]{1,0:T(8,128)(2,1)S(1)} %copy-done.1, bf16[512,512]{1,0:T(8,128)(2,1)S(1)} %copy-done.2, ...), custom_call_target="tpu_custom_call" | custom-call | tf_op jit(solution)/shard_map/whole_step/pallas_call | solution.py:453
  67.4 1.1 %write_results.1 = (bf16[64,512]{1,0:T(8,128)(2,1)}, bf16[1024,512]{1,0:T(8,128)(2,1)}, f32[5,8192]{1,0:T(8,128)}) custom-call(bf16[64,512]{1,0:T(8,128)(2,1)S(1)} %get-tuple-element.9.refs_0_, bf16[1024,512]{1,0:T(8,128)(2,1)S(1)} %get-tuple-element.10.refs_1_, f32[5,8192]{1,0:T(8,128)S(1)} %get-tuple-element.11.refs_2_), custom_call_target="tpu_custom_call" | custom-call | tf_op jit(solution)/shard_map/write_results/pallas_call | solution.py:496
Async XLA Ops:
  0.6 0.7 %copy-start.10 = (s32[8,8,1]{1,2,0:T(1,128)S(1)}, s32[8,8,1]{1,2,0:T(1,128)}, u32[]{:S(2)}) copy-start(s32[8,8,1]{1,2,0:T(1,128)} %param.20) | copy-start | bytes 772
  0.6 0.7 copy-start.11
  1.3 1.2 %copy-start = (bf16[1024,512]{1,0:T(8,128)(2,1)S(1)}, bf16[1024,512]{1,0:T(8,128)(2,1)}, u32[]{:S(2)}) copy-start(bf16[1024,512]{1,0:T(8,128)(2,1)} %refs_1_.1) | copy-start | bytes 3145732
  2.6 1.0 %copy-start.1 = (bf16[512,512]{1,0:T(8,128)(2,1)S(1)}, bf16[512,512]{1,0:T(8,128)(2,1)}, u32[]{:S(2)}) copy-start(bf16[512,512]{1,0:T(8,128)(2,1)} %refs_2_.1) | copy-start | bytes 1572868
  3.6 1.0 %copy-start.2 = (bf16[512,512]{1,0:T(8,128)(2,1)S(1)}, bf16[512,512]{1,0:T(8,128)(2,1)}, u32[]{:S(2)}) copy-start(bf16[512,512]{1,0:T(8,128)(2,1)} %refs_3_.1) | copy-start | bytes 1572868
  4.6 1.0 %copy-start.3 = (bf16[512,512]{1,0:T(8,128)(2,1)S(1)}, bf16[512,512]{1,0:T(8,128)(2,1)}, u32[]{:S(2)}) copy-start(bf16[512,512]{1,0:T(8,128)(2,1)} %refs_4_.1) | copy-start | bytes 1572868
  5.7 1.0 %copy-start.4 = (bf16[512,512]{1,0:T(8,128)(2,1)S(1)}, bf16[512,512]{1,0:T(8,128)(2,1)}, u32[]{:S(2)}) copy-start(bf16[512,512]{1,0:T(8,128)(2,1)} %refs_5_.1) | copy-start | bytes 1572868
  6.7 1.0 %copy-start.5 = (bf16[512,512]{1,0:T(8,128)(2,1)S(1)}, bf16[512,512]{1,0:T(8,128)(2,1)}, u32[]{:S(2)}) copy-start(bf16[512,512]{1,0:T(8,128)(2,1)} %refs_6_.1) | copy-start | bytes 1572868
  7.8 0.8 %copy-start.6 = (bf16[8,8,512]{2,1,0:T(8,128)(2,1)S(1)}, bf16[8,8,512]{2,1,0:T(8,128)(2,1)}, u32[]{:S(2)}) copy-start(bf16[8,8,512]{2,1,0:T(8,128)(2,1)} %param.12) | copy-start | bytes 196612
  8.6 0.7 %copy-start.7 = (s32[6,8,8]{2,1,0:T(8,128)S(1)}, s32[6,8,8]{2,1,0:T(8,128)}, u32[]{:S(2)}) copy-start(s32[6,8,8]{2,1,0:T(8,128)} %refs_7_.1) | copy-start | bytes 4612
  9.3 0.7 %copy-start.8 = (s32[3072]{0:T(1024)S(1)}, s32[3072]{0:T(1024)}, u32[]{:S(2)}) copy-start(s32[3072]{0:T(1024)} %param.21) | copy-start | bytes 36868
  10.0 0.7 %copy-start.9 = (s32[3072]{0:T(1024)S(1)}, s32[3072]{0:T(1024)}, u32[]{:S(2)}) copy-start(s32[3072]{0:T(1024)} %param.22) | copy-start | bytes 36868
